TPU v7x, 32 devices: a whole 2x2x4 slice. The times are simulated.
32 devices in a mesh: seq: 8 (over y, x, core), head: 4 (over z).
Axes of the slice: x: 2, y: 2, z: 4, core: 2. Of those that a mesh axis runs over, the one named last changes fastest.
Arguments:
- frames: bfloat16 [8192, 1024], P(('seq', 'head')), may hold values from -6 to 6
- cotangent: bfloat16 [8192, 1024], P(('seq', 'head')), may hold values from -6 to 6
- norm_gain: float32 [1024], replicated, may hold values from 0.25 to 1.75
- w_qkv: bfloat16 [3, 1024, 1024], replicated
- w_out: bfloat16 [1024, 1024], replicated, may hold values from -0.1875 to 0.1875
Outputs:
- output: bfloat16 [8192, 1024], P(('seq', 'head'))
- grad_frames: bfloat16 [8192, 1024], P(('seq', 'head'))
- grad_qkv: float32 [3, 1024, 1024], P(None, 'seq', 'head')
- grad_out: float32 [1024, 1024], P('seq', 'head')
All inputs are finite; a program needn't handle non-finite values.
Results may differ from a plain program's by a relative error of at most 0.015.
Values may be sent and summed in bfloat16 or wider, within the bound.
A program may use at most 128 MiB of HBM per device.

v0:
```python
import jax
import jax.numpy as jnp
from jax import lax
from jax.sharding import PartitionSpec as P

HEAD_SIZE = 128
WINDOW = 128


EPSILON = 1e-05
MASKED = -1e30


def with_halo(shard, sides, width):
    for axis, dim in sides:
        devices, length = (lax.axis_size(axis), shard.shape[dim])
        up = [(i, (i + 1) % devices) for i in range(devices - 1)]
        down = [(j, i) for i, j in up]
        last = lax.slice_in_dim(shard, length - width, length, axis=dim)
        first = lax.slice_in_dim(shard, 0, width, axis=dim)
        before = lax.ppermute(last, axis, up)
        after = lax.ppermute(first, axis, down)
        shard = jnp.concatenate([before, shard, after], axis=dim)
    return shard


def layer_norm(values, norm_gain):
    average = jnp.mean(values, axis=-1, keepdims=True)
    centered = values - average
    variance = jnp.mean(centered * centered, axis=-1, keepdims=True)
    return centered * lax.rsqrt(variance + EPSILON) * norm_gain


def norm_grad(frames, norm_gain, upstream):
    _, pullback = jax.vjp(lambda v: layer_norm(v, norm_gain), frames.astype(jnp.float32))
    return pullback(upstream.astype(jnp.float32))[0]


def attention(query_rows, key_rows, value_rows, offset, frame_total):
    length, channels = query_rows.shape
    head_count = channels // HEAD_SIZE
    block_rows = min(length, 512)
    block_count = length // block_rows
    key_span = block_rows + 2 * WINDOW
    score_scale = HEAD_SIZE ** (-0.5)

    def one_block(block_index):
        anchor = block_index * block_rows
        query_part = lax.dynamic_slice_in_dim(query_rows, anchor, block_rows, 0).reshape(
            block_rows, head_count, HEAD_SIZE
        )
        key_part = lax.dynamic_slice_in_dim(key_rows, anchor, key_span, 0).reshape(
            key_span, head_count, HEAD_SIZE
        )
        value_part = lax.dynamic_slice_in_dim(value_rows, anchor, key_span, 0).reshape(
            key_span, head_count, HEAD_SIZE
        )
        query_pos = offset + anchor + jnp.arange(block_rows, dtype=jnp.int32)
        key_pos = offset + anchor - WINDOW + jnp.arange(key_span, dtype=jnp.int32)
        distance = query_pos[:, None] - key_pos[None, :]
        allowed = (
            (jnp.abs(distance) <= WINDOW)
            & (key_pos >= 0)[None, :]
            & (key_pos < frame_total)[None, :]
        )
        scores = (
            jnp.einsum("qhe,khe->hqk", query_part, key_part, precision=lax.Precision.HIGHEST)
            * score_scale
        )
        scores = jnp.where(allowed[None], scores, MASKED)
        row_max = lax.stop_gradient(jnp.max(scores, axis=-1, keepdims=True))
        weights = jnp.exp(scores - row_max)
        weights = weights / jnp.sum(weights, axis=-1, keepdims=True)
        combined = jnp.einsum("hqk,khe->qhe", weights, value_part, precision=lax.Precision.HIGHEST)
        return combined.reshape(block_rows, channels)

    results = lax.map(jax.checkpoint(one_block), jnp.arange(block_count, dtype=jnp.int32))
    return results.reshape(length, channels)


def attention_grad(query_rows, key_rows, value_rows, offset, frame_total, upstream):
    _, pullback = jax.vjp(
        lambda a, b, c: attention(a, b, c, offset, frame_total), query_rows, key_rows, value_rows
    )
    return pullback(upstream.astype(jnp.float32))


def to_heads(stacked):
    return lax.all_to_all(stacked, "head", split_axis=2, concat_axis=1, tiled=True)


def to_time(stacked):
    return lax.all_to_all(stacked, "head", split_axis=1, concat_axis=2, tiled=True)


def sum_columns(term):
    return lax.psum_scatter(
        term.astype(jnp.bfloat16), "head", scatter_dimension=2, tiled=True
    ).astype(jnp.float32)


def sum_rows(term):
    return lax.psum_scatter(
        term.astype(jnp.bfloat16), "seq", scatter_dimension=1, tiled=True
    ).astype(jnp.float32)


def shards(frames, cotangent, norm_gain, w_qkv, w_out):
    frame_rows = frames.shape[0]
    head_groups = lax.axis_size("head")
    frame_total = lax.axis_size("seq") * head_groups * frame_rows
    grad_scale = frame_total ** (-0.5)
    normed = layer_norm(frames.astype(jnp.float32), norm_gain).astype(jnp.bfloat16)
    projected = jnp.einsum("td,cdf->ctf", normed, w_qkv, preferred_element_type=jnp.float32).astype(
        jnp.bfloat16
    )
    offset = lax.axis_index("seq") * (head_groups * frame_rows)
    local_qkv = to_heads(projected)
    bordered = with_halo(local_qkv[1:], (("seq", 1),), WINDOW)
    query_rows = local_qkv[0].astype(jnp.float32)
    key_rows = bordered[0].astype(jnp.float32)
    value_rows = bordered[1].astype(jnp.float32)
    length = query_rows.shape[0]
    attended = attention(query_rows, key_rows, value_rows, offset, frame_total).astype(jnp.bfloat16)
    mixed_rows = to_time(attended[None])[0]
    output = (
        frames.astype(jnp.float32) + jnp.dot(mixed_rows, w_out, preferred_element_type=jnp.float32)
    ).astype(jnp.bfloat16)
    grad_mixed = jnp.einsum(
        "tf,df->td", cotangent, w_out, preferred_element_type=jnp.float32
    ).astype(jnp.bfloat16)
    grad_attended = to_heads(grad_mixed[None])[0]
    grad_query, grad_keys, grad_values = attention_grad(
        query_rows, key_rows, value_rows, offset, frame_total, grad_attended
    )
    pair_grads = jnp.stack([grad_keys, grad_values])
    edge_grads = jnp.concatenate([pair_grads[:, :WINDOW], pair_grads[:, length + WINDOW :]], axis=1)
    returned = with_halo(edge_grads.astype(jnp.bfloat16), (("seq", 1),), WINDOW).astype(
        edge_grads.dtype
    )
    interior = pair_grads[:, WINDOW : length + WINDOW]
    interior = interior.at[:, :WINDOW].add(returned[:, :WINDOW])
    interior = interior.at[:, length - WINDOW :].add(returned[:, 3 * WINDOW :])
    grad_local = jnp.concatenate([grad_query[None], interior], axis=0).astype(jnp.bfloat16)
    grad_time = to_time(grad_local)
    grad_normed = jnp.einsum(
        "ctf,cdf->td", grad_time, w_qkv, preferred_element_type=jnp.float32
    ).astype(jnp.bfloat16)
    grad_frames = (
        cotangent.astype(jnp.float32) + norm_grad(frames, norm_gain, grad_normed)
    ).astype(jnp.bfloat16)
    out_term = (
        jnp.einsum("td,tf->df", mixed_rows, cotangent, preferred_element_type=jnp.float32)[None]
        * grad_scale
    )
    grad_out = sum_rows(sum_columns(out_term))[0]
    time_term = (
        jnp.einsum("td,ctf->cdf", normed, grad_time, preferred_element_type=jnp.float32)
        * grad_scale
    )
    grad_qkv = sum_rows(sum_columns(time_term))
    return (output, grad_frames, grad_qkv, grad_out)


def solution(mesh):
    in_specs = (P(("seq", "head"), None), P(("seq", "head"), None), P(), P(), P())
    out_specs = (
        P(("seq", "head"), None),
        P(("seq", "head"), None),
        P(None, "seq", "head"),
        P("seq", "head"),
    )
    return jax.shard_map(shards, mesh=mesh, in_specs=in_specs, out_specs=out_specs, check_vma=False)
```

profile of v0, /device:TPU:0, one launch (start us, length us, event | category | flops | bytes accessed | tf_op | source)
XLA Modules:
  0.0 544.6 jit_solution(4253332027485808211)
XLA Ops:
  13.1 4.8 reduce.5
  18.9 6.3 %all-to-all-start.2 = ((bf16[4,2,32768]{2,1,0:T(2,128)(2,1)}), bf16[4,2,32768]{2,1,0:T(2,128)(2,1)S(1)}, u32[]{:S(2)}, u32[]{:S(2)}) async-start(bf16[4,2,32768]{2,1,0:T(2,128)(2,1)} %reshape.388), calls=%async_computation.2 | async-start | bytes 1048576 | tf_op jit(solution)/shard_map/all_to_all | solution.py:89
  26.8 5.9 %fusion.34 = bf16[3,256,1024]{2,1,0:T(8,128)(2,1)} fusion(bf16[3,1024,1024]{2,1,0:T(8,128)(2,1)} %param.16, bf16[256,1024]{1,0:T(8,128)(2,1)S(1)} %copy-done.13, f32[1024]{0:T(1024)S(1)} %copy-done.28, f32[256]{0:T(256)S(1)} %fusion.53, f32[256]{0:T(256)S(1)} %broadcast_multiply_fusion), kind=kOutput, calls=%fused_computation.76 | convolution fusion | flops 1612709888 | bytes 8394752 | tf_op jit(solution)/shard_map/td,cdf->ctf/dot_general | solution.py:114
  32.6 4.1 copy.107
  39.7 4.5 all-to-all-start
  47.9 44.0 %all-to-all-done = bf16[3,256,1024]{1,0,2:T(4,128)(2,1)} async-done(((bf16[3,256,1024]{1,0,2:T(4,128)(2,1)}), bf16[3,256,1024]{1,0,2:T(4,128)(2,1)}, u32[]{:S(2)}, u32[]{:S(2)}) %all-to-all-start) | async-done | bytes 1572896 | tf_op jit(solution)/shard_map/all_to_all | solution.py:89
  92.0 4.1 copy.109
  111.7 29.2 %while.32 = (s32[]{:T(128)}, bf16[2,512,256]{2,1,0:T(8,128)(2,1)}, s32[2]{0:T(128)S(1)}, f32[1280,256]{0,1:T(8,128)}, s32[]{:T(128)}, /*index=5*/f32[1024,256]{0...) while((s32[]{:T(128)}, bf16[2,512,256]{2,1,0:T(8,128)(2,1)}, ...), condition=%wide.region_5.6_spmd, body=%wide.region_2.5_spmd.sunk | while | flops 2426537472 | bytes 25986388 | solution.py:77
  117.1 3.3 fusion.114
  121.3 4.1 fusion.116
  131.7 3.3 fusion.114
  135.9 4.1 fusion.116
  142.8 4.7 reduce.4
  149.4 4.1 all-to-all-start.1
  157.0 70.9 %while.33 = (s32[]{:T(128)}, f32[1024,256]{1,0:T(8,128)}, f32[1280,256]{0,1:T(8,128)}, f32[1280,256]{0,1:T(8,128)}, s32[2]{0:T(128)S(1)}, /*index=5*/f32[2,512,2...) while((s32[]{:T(128)}, f32[1024,256]{1,0:T(8,128)}, ...), condition=%wide.region_10.11_spmd, body=%wide.region_6.10_spmd.sunk | while | flops 6061953024 | bytes 89728512 | solution.py:77
  175.2 3.3 fusion.130
  179.6 3.9 multiply_reduce_fusion.2
  189.9 3.4 fusion.132
  208.9 3.9 multiply_reduce_fusion.2
  219.2 3.4 fusion.132
  227.9 3.9 copy.138
  238.3 3.3 fusion.29
  241.7 4.1 fusion.27
  245.9 4.8 collective-permute-start.2
  258.9 74.3 %all_to_all.57 = bf16[3,1024,256]{2,0,1:T(4,128)(2,1)S(1)} all-to-all(bf16[3,1024,256]{2,0,1:T(4,128)(2,1)S(1)} %pad_maximum_fusion.1), channel_id=1, replica_groups=mesh['seq'=8,'head'=4] {'head'}, dimensions={1} | all-to-all | bytes 3145728 | tf_op jit(solution)/shard_map/all_to_all | solution.py:93
  335.9 3.8 all_to_all.52
  339.7 6.1 %fusion.26 = bf16[3,1024,1024]{1,2,0:T(8,128)(2,1)} fusion(bf16[3,256,1024]{2,1,0:T(8,128)(2,1)} %all_to_all.52, bf16[256,1024]{1,0:T(8,128)(2,1)S(1)} %copy-done.14, f32[1024]{0:T(1024)S(1)} %copy-done.29, f32[256]{0:T(256)S(1)} %copy-done.25, f32[256]{0:T(256)S(1)} %copy-done.23), kind=kOutput, calls=%fused_computation.55 | convolution fusion | flops 1618214912 | bytes 8394752 | tf_op jit(solution)/shard_map/td,ctf->cdf/dot_general | solution.py:158
  346.6 109.6 %reduce-scatter.7.cloned.1.call-done = bf16[3,1024,256]{1,2,0:T(8,128)(2,1)} async-done(((bf16[3,1024,1024]{1,2,0:T(8,128)(2,1)}), bf16[3,1024,256]{1,2,0:T(8,128)(2,1)}) %reduce-scatter.7.cloned.1.call-update) | async-done | bytes 1572880 | tf_op jit(solution)/shard_map/reduce_scatter | solution.py:97
  456.2 4.4 copy.140
  465.3 5.1 fusion.43
  472.0 21.9 %reduce-scatter.11.cloned.1.call-done = bf16[1,128,256]{2,1,0:T(8,128)(2,1)} async-done(((bf16[1,1024,256]{2,1,0:T(8,128)(2,1)}), bf16[1,128,256]{2,1,0:T(8,128)(2,1)}) %reduce-scatter.11.cloned.1.call-update) | async-done | bytes 65552 | tf_op jit(solution)/shard_map/reduce_scatter | solution.py:103
  495.5 40.1 %reduce-scatter.13.cloned.1.call-done = bf16[128,768]{1,0:T(8,128)(2,1)} async-done(((bf16[1024,768]{1,0:T(8,128)(2,1)}), bf16[128,768]{1,0:T(8,128)(2,1)}) %reduce-scatter.13.cloned.1.call-update) | async-done | bytes 196624
  (216 shorter events, 118.3 us)
Async XLA Ops:
  10.5 14.7 %copy-start.13 = (bf16[256,1024]{1,0:T(8,128)(2,1)S(1)}, bf16[256,1024]{1,0:T(8,128)(2,1)}, u32[]{:S(2)}) copy-start(bf16[256,1024]{1,0:T(8,128)(2,1)} %param.13) | copy-start | bytes 1572868
  10.6 16.2 %copy-start.28 = (f32[1024]{0:T(1024)S(1)}, f32[1024]{0:T(1024)}, u32[]{:S(2)}) copy-start(f32[1024]{0:T(1024)} %param.15) | copy-start | bytes 12292
  18.9 20.8 %all-to-all-start.2 = ((bf16[4,2,32768]{2,1,0:T(2,128)(2,1)}), bf16[4,2,32768]{2,1,0:T(2,128)(2,1)S(1)}, u32[]{:S(2)}, u32[]{:S(2)}) async-start(bf16[4,2,32768]{2,1,0:T(2,128)(2,1)} %reshape.388), calls=%async_computation.2 | async-start | bytes 1048576 | tf_op jit(solution)/shard_map/all_to_all | solution.py:89
  39.7 4.5 copy-start.17
  39.7 52.3 %all-to-all-start = ((bf16[3,256,1024]{1,0,2:T(4,128)(2,1)}), bf16[3,256,1024]{1,0,2:T(4,128)(2,1)}, u32[]{:S(2)}, u32[]{:S(2)}) async-start(bf16[3,256,1024]{1,0,2:T(4,128)(2,1)} %copy.107), calls=%async_computation | async-start | bytes 4194304 | tf_op jit(solution)/shard_map/all_to_all | solution.py:89
  102.4 7.5 %collective-permute-start = (bf16[2,128,256]{1,2,0:T(8,128)(2,1)}, bf16[2,128,256]{1,2,0:T(8,128)(2,1)S(1)}, u32[]{:S(2)}, u32[]{:S(2)}) collective-permute-start(bf16[2,128,256]{1,2,0:T(8,128)(2,1)} %get-tuple-element.473), channel_id=1, source_target_pairs={{0,4},{4,8},{8,12},{12,16},{16,20},{20,24},{24,28},{1,5},{5,9},{9,... | collective-permute-start | bytes 393224 | tf_op jit(solution)/shard_map/ppermute | solution.py:21
  103.7 6.2 %collective-permute-start.1 = (bf16[2,128,256]{1,2,0:T(8,128)(2,1)S(1)}, bf16[2,128,256]{1,2,0:T(8,128)(2,1)S(1)}, u32[]{:S(2)}, u32[]{:S(2)}) collective-permute-start(bf16[2,128,256]{1,2,0:T(8,128)(2,1)S(1)} %get-tuple-element.474), channel_id=1, source_target_pairs={{4,0},{8,4},{12,8},{16,12},{20,16},{24,20},{28,24},{5,1},{9,5},{13... | collective-permute-start | bytes 393224 | tf_op jit(solution)/shard_map/ppermute | solution.py:22
  117.0 4.2 copy-start.12
  121.3 4.2 copy-start.20
  131.7 4.2 copy-start.12
  135.9 4.2 copy-start.20
  149.4 84.5 %all-to-all-start.1 = ((bf16[4,2,32768]{2,1,0:T(2,128)(2,1)}), bf16[4,2,32768]{2,1,0:T(2,128)(2,1)}, u32[]{:S(2)}, u32[]{:S(2)}) async-start(bf16[4,2,32768]{2,1,0:T(2,128)(2,1)} %reshape.390), calls=%async_computation.1 | async-start | bytes 1048576 | tf_op jit(solution)/shard_map/all_to_all | solution.py:93
  153.6 192.3 %reduce-scatter.9.cloned.1.call-start = ((), (), s32[]{:S(2)}) async-start(), calls=%async_computation.9 | async-start | bytes 2621440 | tf_op jit(solution)/shard_map/reduce_scatter | solution.py:97
  175.2 4.2 copy-start.1
  189.8 3.4 copy-start.4
  189.9 3.4 copy-start.6
  204.6 4.2 copy-start.1
  227.9 3.9 copy-start.7
  241.6 10.4 %copy-start.9 = (f32[1024,256]{1,0:T(8,128)S(1)}, f32[1024,256]{1,0:T(8,128)}, u32[]{:S(2)}) copy-start(f32[1024,256]{1,0:T(8,128)} %get-tuple-element.325) | copy-start | bytes 3145732
  241.6 214.6 %reduce-scatter.7.cloned.1.call-start = ((), (), s32[]{:S(2)}) async-start(), calls=%async_computation.8 | async-start | bytes 7864320 | tf_op jit(solution)/shard_map/reduce_scatter | solution.py:97
  241.7 11.2 %copy-start.10 = (f32[1,1280,256]{2,0,1:T(1,128)S(1)}, f32[1,1280,256]{2,0,1:T(1,128)}, u32[]{:S(2)}) copy-start(f32[1,1280,256]{2,0,1:T(1,128)} %copy.138) | copy-start | bytes 3932164
  241.7 11.2 %copy-start.11 = (f32[1,1280,256]{2,0,1:T(1,128)S(1)}, f32[1,1280,256]{2,0,1:T(1,128)}, u32[]{:S(2)}) copy-start(f32[1,1280,256]{2,0,1:T(1,128)} %copy.139) | copy-start | bytes 3932164
  245.9 8.9 %collective-permute-start.2 = (bf16[2,128,256]{2,0,1:T(2,128)(2,1)S(1)}, bf16[2,128,256]{2,0,1:T(2,128)(2,1)S(1)}, u32[]{:S(2)}, u32[]{:S(2)}) collective-permute-start(bf16[2,128,256]{2,0,1:T(2,128)(2,1)S(1)} %get-tuple-element.469), channel_id=1, source_target_pairs={{0,4},{4,8},{8,12},{12,16},{16,20},{20,24},{24,28},{1,5},{5,9},{9,... | collective-permute-start | bytes 393224 | tf_op jit(solution)/shard_map/ppermute | solution.py:21
  250.7 4.5 collective-permute-start.3
  333.2 6.5 %copy-start.14 = (bf16[256,1024]{1,0:T(8,128)(2,1)S(1)}, bf16[256,1024]{1,0:T(8,128)(2,1)}, u32[]{:S(2)}) copy-start(bf16[256,1024]{1,0:T(8,128)(2,1)} %param.13) | copy-start | bytes 1572868
  333.2 6.5 %copy-start.23 = (f32[256]{0:T(256)S(1)}, f32[256]{0:T(256)}, u32[]{:S(2)}) copy-start(f32[256]{0:T(256)} %copy-done.22) | copy-start | bytes 3076
  333.2 6.5 %copy-start.25 = (f32[256]{0:T(256)S(1)}, f32[256]{0:T(256)}, u32[]{:S(2)}) copy-start(f32[256]{0:T(256)} %copy-done.24) | copy-start | bytes 3076
  333.2 6.5 %copy-start.29 = (f32[1024]{0:T(1024)S(1)}, f32[1024]{0:T(1024)}, u32[]{:S(2)}) copy-start(f32[1024]{0:T(1024)} %param.15) | copy-start | bytes 12292
  345.8 148.2 %reduce-scatter.11.cloned.1.call-start = ((), (), s32[]{:S(2)}) async-start(), calls=%async_computation.10 | async-start | bytes 589824 | tf_op jit(solution)/shard_map/reduce_scatter | solution.py:103
  346.5 189.0 %reduce-scatter.13.cloned.1.call-start = ((), (), s32[]{:S(2)}) async-start(), calls=%async_computation.11 | async-start | bytes 1769472
  465.3 5.1 copy-start.27
  465.3 5.5 %copy-start.18 = (bf16[256,1024]{1,0:T(8,128)(2,1)S(1)}, bf16[256,1024]{1,0:T(8,128)(2,1)}, u32[]{:S(2)}) copy-start(bf16[256,1024]{1,0:T(8,128)(2,1)} %param.14) | copy-start | bytes 1572868
  (19 other events, 40.2 us)
Sparse Core Ops, SparseCore 0:
  241.7 66.6 reduce-scatter.8
  345.9 110.2 reduce-scatter.6
  459.3 34.6 reduce-scatter.10
  497.1 38.3 reduce-scatter.12
where the time goes:
time: 553 us; the launch traced here: 545 us
  waiting for transfers between devices  220 us (40%)
  local copies, waits for them, and re-layouts  90.1 us (16%)
  blocking collectives  74.3 us (13%)
  matrix products  68.8 us (12%)
  other arithmetic  37.8 us (7%)
  starting transfers between devices  24 us (4%)
  loops' own time  15.4 us (3%)
  between operations  14.6 us (3%)
    reduce_scatter x2, waiting for transfers between devices, sum_columns(): lax.psum_scatter(term.astype(jnp.bfloat16), 'head', scatter_dimension=2,...  110 us
    all_to_all x1, blocking collectives, to_time(): lax.all_to_all(stacked, 'head', split_axis=1, concat_axis=2, tiled=True)  74.3 us
    all_to_all x2, waiting for transfers between devices, to_heads(): lax.all_to_all(stacked, 'head', split_axis=2, concat_axis=1, tiled=True)  47 us
    unnamed x5, waiting for transfers between devices  40.8 us
    dot_general x8, matrix products, one_block(): jnp.einsum('qhe,khe->hqk', query_part, key_part, precision=lax.Precision....  23.7 us
    reduce_scatter x1, waiting for transfers between devices, sum_rows(): lax.psum_scatter(term.astype(jnp.bfloat16), 'seq', scatter_dimension=1, t...  21.9 us
    dot_general x6, matrix products, one_block(): jnp.einsum('hqk,khe->qhe', weights, value_part, precision=lax.Precision.H...  21.4 us
    unnamed x51, local copies, waits for them, and re-layouts  21.2 us
  transfers between devices with their start and end apart: 11, of which 6 were waited for; matrix products, arithmetic and copies ran while one was open for 22% of the time, Pallas kernels for 0%

commit v1 on v0

v1 whole, which is shorter than its diff:
```python
import functools

import jax
import jax.numpy as jnp
from jax import lax
from jax.experimental import pallas as pl
from jax.experimental.pallas import tpu as pltpu
from jax.sharding import PartitionSpec as P

HEAD_SIZE = 128
WINDOW = 128

EPSILON = 1e-05
MASKED = -1e30
AXES = ("seq", "head")


def layer_norm(values, norm_gain):
    average = jnp.mean(values, axis=-1, keepdims=True)
    centered = values - average
    variance = jnp.mean(centered * centered, axis=-1, keepdims=True)
    return centered * lax.rsqrt(variance + EPSILON) * norm_gain


def norm_grad(frames, norm_gain, upstream):
    _, pullback = jax.vjp(lambda v: layer_norm(v, norm_gain), frames.astype(jnp.float32))
    return pullback(upstream.astype(jnp.float32))[0]


def shift(rows, step):
    devices = lax.axis_size("seq") * lax.axis_size("head")
    pairs = [(i, i + step) for i in range(devices) if 0 <= i + step < devices]
    return lax.ppermute(rows, AXES, pairs)


def dot(a, b, contract):
    return lax.dot_general(a, b, (contract, ((), ())), preferred_element_type=jnp.float32)


def attention_kernel(heads, offset_ref, q_ref, k_ref, v_ref, up_ref, out_ref, dq_ref, mid_ref, edge_ref):
    length = q_ref.shape[0]
    blocks = length // WINDOW
    span = 3 * WINDOW
    scale = HEAD_SIZE ** (-0.5)
    offset, total = offset_ref[0], offset_ref[1]
    row = lax.broadcasted_iota(jnp.int32, (WINDOW, span), 0)
    col = lax.broadcasted_iota(jnp.int32, (WINDOW, span), 1)
    near = (col >= row) & (col <= row + 2 * WINDOW)
    for head in range(heads):
        lanes = slice(head * HEAD_SIZE, (head + 1) * HEAD_SIZE)
        key_grads = [None] * (blocks + 2)
        value_grads = [None] * (blocks + 2)
        for block in range(blocks):
            rows = slice(block * WINDOW, (block + 1) * WINDOW)
            keys = slice(block * WINDOW, block * WINDOW + span)
            q, k, v = q_ref[rows, lanes], k_ref[keys, lanes], v_ref[keys, lanes]
            up = up_ref[rows, lanes]
            position = offset + (block - 1) * WINDOW + col
            allowed = near & (position >= 0) & (position < total)
            scores = jnp.where(allowed, dot(q, k, ((1,), (1,))) * scale, MASKED)
            weights = jnp.exp(scores - jnp.max(scores, axis=-1, keepdims=True))
            weights = weights / jnp.sum(weights, axis=-1, keepdims=True)
            rounded = weights.astype(jnp.bfloat16)
            out_ref[rows, lanes] = dot(rounded, v, ((1,), (0,))).astype(jnp.bfloat16)
            grad = dot(up, v, ((1,), (1,)))
            centre = jnp.sum(weights * grad, axis=-1, keepdims=True)
            grad = (weights * (grad - centre) * scale).astype(jnp.bfloat16)
            dq_ref[rows, lanes] = dot(grad, k, ((1,), (0,))).astype(jnp.bfloat16)
            key_grad = dot(grad, q, ((0,), (0,)))
            value_grad = dot(rounded, up, ((0,), (0,)))
            for part in range(3):
                piece = slice(part * WINDOW, (part + 1) * WINDOW)
                for sums, term in ((key_grads, key_grad[piece]), (value_grads, value_grad[piece])):
                    held = sums[block + part]
                    sums[block + part] = term if held is None else held + term
        for which, sums in enumerate((key_grads, value_grads)):
            edge_ref[which, :WINDOW, lanes] = sums[0].astype(jnp.bfloat16)
            edge_ref[which, WINDOW:, lanes] = sums[-1].astype(jnp.bfloat16)
            for block in range(blocks):
                mid_ref[which, block * WINDOW : (block + 1) * WINDOW, lanes] = sums[block + 1]


def attention(query, key, value, upstream, offset, total):
    length, channels = query.shape
    heads = 2
    wide = heads * HEAD_SIZE
    bordered = key.shape[0]

    def rows_spec(rows):
        return pl.BlockSpec((rows, wide), lambda i: (0, i))

    def pair_spec(rows):
        return pl.BlockSpec((2, rows, wide), lambda i: (0, 0, i))

    return pl.pallas_call(
        functools.partial(attention_kernel, heads),
        grid=(channels // wide,),
        in_specs=[
            pl.BlockSpec(memory_space=pltpu.SMEM),
            rows_spec(length),
            rows_spec(bordered),
            rows_spec(bordered),
            rows_spec(length),
        ],
        out_specs=[rows_spec(length), rows_spec(length), pair_spec(length), pair_spec(2 * WINDOW)],
        out_shape=[
            jax.ShapeDtypeStruct((length, channels), jnp.bfloat16),
            jax.ShapeDtypeStruct((length, channels), jnp.bfloat16),
            jax.ShapeDtypeStruct((2, length, channels), jnp.float32),
            jax.ShapeDtypeStruct((2, 2 * WINDOW, channels), jnp.bfloat16),
        ],
        name="attention",
    )(jnp.stack([offset, jnp.int32(total)]), query, key, value, upstream)


def bits_of(size):
    return list(range(size.bit_length() - 1))


def scatter_kernel(chunks, orders, sizes, scale, *refs):
    left, right = refs[:chunks], refs[chunks : 2 * chunks]
    out_ref, held, landed, send_sem, recv_sem = refs[2 * chunks :]
    seq_size, head_size = sizes
    tiles = seq_size * head_size
    place = {axis: lax.axis_index(axis) for axis in AXES}
    stages = len(orders[0])
    tile_rows, tile_cols = held.shape[2:]

    def bit_at(order):
        axis, bit = order
        return (place[axis] // 2**bit) % 2

    def partner(order):
        axis, bit = order
        moved = place[axis] + (1 - 2 * bit_at(order)) * 2**bit
        return tuple(moved if name == axis else place[name] for name in AXES)

    barrier = pltpu.get_barrier_semaphore()
    for order in orders[0]:
        pl.semaphore_signal(
            barrier, inc=1, device_id=partner(order), device_id_type=pl.DeviceIdType.MESH
        )
    pl.semaphore_wait(barrier, stages)

    def base(chunk, stage):
        total = 0
        for step in range(stage):
            total = total + bit_at(orders[chunk][step]) * (tiles >> (step + 1))
        return total

    def landing(stage):
        return tiles - (tiles >> stage)

    def copy(chunk, stage):
        half = tiles >> (stage + 1)
        order = orders[chunk][stage]
        other = base(chunk, stage) + (1 - bit_at(order)) * half
        return pltpu.make_async_remote_copy(
            src_ref=held.at[chunk, pl.ds(other, half)],
            dst_ref=landed.at[chunk, pl.ds(landing(stage), half)],
            send_sem=send_sem.at[chunk, stage],
            recv_sem=recv_sem.at[chunk, stage],
            device_id=partner(order),
            device_id_type=pl.DeviceIdType.MESH,
        )

    def finish(chunk, stage):
        copy(chunk, stage).wait()
        half = tiles >> (stage + 1)
        keep = base(chunk, stage + 1)
        if stage == stages - 1:
            own = held[chunk, keep].astype(jnp.float32)
            own = own + landed[chunk, landing(stage)].astype(jnp.float32)
            out_ref[chunk] = own * scale
            return

        def add(step, carry):
            own = held[chunk, keep + step].astype(jnp.float32)
            own = own + landed[chunk, landing(stage) + step].astype(jnp.float32)
            held[chunk, keep + step] = own.astype(jnp.bfloat16)
            return carry

        lax.fori_loop(0, half, add, 0)

    def column_place(chunk, col):
        total = 0
        for step, (axis, bit) in enumerate(orders[chunk]):
            if axis == "head":
                total += ((col >> bit) & 1) * (tiles >> (step + 1))
        return total

    def multiply(chunk, half):
        seq_steps = [bit for axis, bit in orders[chunk] if axis == "seq"]

        def one(step, carry):
            slot = half * (seq_size // 2) + step
            row_block = 0
            for depth, bit in enumerate(seq_steps):
                row_block = row_block + ((slot // (seq_size >> (depth + 1))) % 2) * 2**bit
            product = dot(left[chunk][row_block], right[chunk][...], ((1,), (0,))).astype(jnp.bfloat16)
            for col in range(head_size):
                held[chunk, slot * head_size + column_place(chunk, col)] = product[
                    :, col * tile_cols : (col + 1) * tile_cols
                ]
            return carry

        lax.fori_loop(0, seq_size // 2, one, 0)

    for wave in range(chunks + stages):
        for chunk in range(chunks - 1, -1, -1):
            stage = wave - chunk
            if stage == 0:
                mine = bit_at(orders[chunk][0])
                multiply(chunk, 1 - mine)
                copy(chunk, 0).start()
                multiply(chunk, mine)
            elif 0 < stage <= stages:
                finish(chunk, stage - 1)
                if stage < stages:
                    copy(chunk, stage).start()


def scatter_products(left, right, collective_id, scale):
    seq_size, head_size = lax.axis_size("seq"), lax.axis_size("head")
    chunks = len(left)
    depth, cols = right[0].shape
    rows = left[0].shape[0]
    tile_rows, tile_cols = rows // seq_size, cols // head_size
    tiles = seq_size * head_size
    seq_bits, head_bits = bits_of(seq_size), bits_of(head_size)
    tail = [("head", bit) for bit in reversed(head_bits)]
    orders = []
    for chunk in range(chunks):
        outer = seq_bits[1:] if chunk % 2 == 0 else seq_bits[:0:-1]
        orders.append([("seq", bit) for bit in seq_bits[:1] + outer] + tail)
    stages = len(orders[0])
    blocks = [term.reshape(seq_size, tile_rows, depth) for term in left]
    vmem = pl.BlockSpec(memory_space=pltpu.VMEM)
    return pl.pallas_call(
        functools.partial(scatter_kernel, chunks, orders, (seq_size, head_size), scale),
        out_shape=jax.ShapeDtypeStruct((chunks, tile_rows, tile_cols), jnp.float32),
        in_specs=[vmem] * (2 * chunks),
        out_specs=vmem,
        scratch_shapes=[
            pltpu.VMEM((chunks, tiles, tile_rows, tile_cols), jnp.bfloat16),
            pltpu.VMEM((chunks, tiles, tile_rows, tile_cols), jnp.bfloat16),
            pltpu.SemaphoreType.DMA((chunks, stages)),
            pltpu.SemaphoreType.DMA((chunks, stages)),
        ],
        compiler_params=pltpu.CompilerParams(collective_id=collective_id, has_side_effects=True),
        cost_estimate=pl.CostEstimate(
            flops=2 * chunks * rows * depth * cols,
            bytes_accessed=20 * chunks * rows * cols,
            transcendentals=0,
        ),
        name="scatter_products_%d" % collective_id,
    )(*blocks, *right)


def shards(frames, cotangent, norm_gain, w_qkv, w_out):
    length = frames.shape[0]
    position = lax.axis_index("seq") * lax.axis_size("head") + lax.axis_index("head")
    frame_total = lax.axis_size("seq") * lax.axis_size("head") * length
    grad_scale = frame_total ** (-0.5)
    before = shift(frames[length - WINDOW :], 1)
    after = shift(frames[:WINDOW], -1)
    upstream = dot(cotangent, w_out, ((1,), (1,))).astype(jnp.bfloat16)
    bordered = jnp.concatenate([before, frames, after], axis=0)
    normed_all = layer_norm(bordered.astype(jnp.float32), norm_gain).astype(jnp.bfloat16)
    normed = normed_all[WINDOW : WINDOW + length]
    query = dot(normed, w_qkv[0], ((1,), (0,))).astype(jnp.bfloat16)
    key = dot(normed_all, w_qkv[1], ((1,), (0,))).astype(jnp.bfloat16)
    value = dot(normed_all, w_qkv[2], ((1,), (0,))).astype(jnp.bfloat16)
    attended, grad_query, pair_grads, edges = attention(
        query, key, value, upstream, position * length, frame_total
    )
    from_next = shift(edges[:, :WINDOW], -1)
    from_previous = shift(edges[:, WINDOW:], 1)
    normed_t = normed.T
    first = scatter_products([attended.T, normed_t], [cotangent, grad_query], 0, grad_scale)
    output = (frames.astype(jnp.float32) + dot(attended, w_out, ((1,), (0,)))).astype(jnp.bfloat16)
    pair_grads = pair_grads.at[:, :WINDOW].add(from_previous.astype(jnp.float32))
    pair_grads = pair_grads.at[:, length - WINDOW :].add(from_next.astype(jnp.float32))
    grad_key, grad_value = pair_grads[0].astype(jnp.bfloat16), pair_grads[1].astype(jnp.bfloat16)
    second = scatter_products([normed_t, normed_t], [grad_key, grad_value], 1, grad_scale)
    grad_normed = (
        dot(grad_query, w_qkv[0], ((1,), (1,)))
        + dot(grad_key, w_qkv[1], ((1,), (1,)))
        + dot(grad_value, w_qkv[2], ((1,), (1,)))
    ).astype(jnp.bfloat16)
    grad_frames = (
        cotangent.astype(jnp.float32) + norm_grad(frames, norm_gain, grad_normed)
    ).astype(jnp.bfloat16)
    grad_qkv = jnp.concatenate([first[1:], second], axis=0)
    return (output, grad_frames, grad_qkv, first[0])


def solution(mesh):
    in_specs = (P(("seq", "head"), None), P(("seq", "head"), None), P(), P(), P())
    out_specs = (
        P(("seq", "head"), None),
        P(("seq", "head"), None),
        P(None, "seq", "head"),
        P("seq", "head"),
    )
    return jax.shard_map(shards, mesh=mesh, in_specs=in_specs, out_specs=out_specs, check_vma=False)
```

time: 553 us -> 169 us (0.31); the launches traced: 545 us -> 169 us
  waiting for transfers between devices: 220 us -> 9.13 us
  Pallas kernels: 0 us -> 105 us
  local copies, waits for them, and re-layouts: 90.1 us -> 12.3 us
  blocking collectives: 74.3 us -> 0 us
  matrix products: 68.8 us -> 18.6 us
  other arithmetic: 37.8 us -> 10.1 us
  loops' own time: 15.4 us -> 0 us
  between operations: 14.6 us -> 0.84 us
  starting transfers between devices: 24 us -> 13 us
    reduce_scatter x3 -> x0, waiting for transfers between devices: 132 us -> none  [the longest x2 110 us: sum_columns(): lax.psum_scatter(term.astype(jnp.bfloat16), 'head', scatter_dimension=2,...]
    pallas_call x0 -> x3, Pallas kernels: none -> 105 us  [the longest x2 90.9 us: scatter_products(): pl.pallas_call(functools.partial(scatter_kernel, chunks, orders, (seq_siz...]
    all_to_all x1 -> x0, blocking collectives: 74.3 us -> none  [to_time(): lax.all_to_all(stacked, 'head', split_axis=1, concat_axis=2, tiled=True)]
    dot_general x20 -> x8, matrix products: 68.8 us -> 18.6 us  [dot(): lax.dot_general(a, b, (contract, ((), ())), preferred_element_type=jnp.fl...]
    all_to_all x3 -> x0, waiting for transfers between devices: 47 us -> none  [the longest x2 47 us: to_heads(): lax.all_to_all(stacked, 'head', split_axis=2, concat_axis=1, tiled=True)]
    unnamed x5 -> x0, waiting for transfers between devices: 40.8 us -> none
    unnamed x51 -> x22, local copies, waits for them, and re-layouts: 21.2 us -> 0.86 us
    dynamic_slice x18 -> x0, local copies, waits for them, and re-layouts: 18 us -> none  [the longest x4 7.11 us: one_block(): lax.dynamic_slice_in_dim(key_rows, anchor, key_span, 0)]
  transfers between devices with their start and end apart: 11 -> 4, of which waited for: 6 -> 2; matrix products, arithmetic and copies ran while one was open for 22% -> 6% of each run, Pallas kernels for 0% -> 27%
where the time goes in v1:
time: 169 us
  Pallas kernels  105 us (62%)
  matrix products  18.6 us (11%)
  starting transfers between devices  13 us (8%)
  local copies, waits for them, and re-layouts  12.3 us (7%)
  other arithmetic  10.1 us (6%)
  waiting for transfers between devices  9.13 us (5%)
    pallas_call x2, Pallas kernels, scatter_products(): pl.pallas_call(functools.partial(scatter_kernel, chunks, orders, (seq_siz...  90.9 us
    dot_general x8, matrix products, dot(): lax.dot_general(a, b, (contract, ((), ())), preferred_element_type=jnp.fl...  18.6 us
    pallas_call x1, Pallas kernels, attention(): pl.pallas_call(functools.partial(attention_kernel, heads), grid=(channels...  13.6 us
    ppermute x4, starting transfers between devices, shift(): return lax.ppermute(rows, AXES, pairs)  13 us
    ppermute x4, waiting for transfers between devices, shift(): return lax.ppermute(rows, AXES, pairs)  9.13 us
  transfers between devices with their start and end apart: 4, of which 2 were waited for; matrix products, arithmetic and copies ran while one was open for 6% of the time, Pallas kernels for 27%

profile of v1, /device:TPU:0, one launch (start us, length us, event | category | flops | bytes accessed | tf_op | source)
XLA Modules:
  0.0 168.5 jit_solution(765379984948756536)
XLA Ops:
  0.6 1.9 %fusion.60 = (bf16[128,1024]{1,0:T(8,128)(2,1)}, bf16[128,1024]{1,0:T(8,128)(2,1)S(1)}) fusion(bf16[256,1024]{1,0:T(8,128)(2,1)} %param.9), kind=kLoop, calls=%fused_computation.67 | loop fusion | bytes 1048576 | tf_op jit(solution)/shard_map/slice | solution.py:265
  2.6 5.1 %collective-permute-start = (bf16[128,1024]{1,0:T(8,128)(2,1)}, bf16[128,1024]{1,0:T(8,128)(2,1)S(1)}, u32[]{:S(2)}, u32[]{:S(2)}) collective-permute-start(bf16[128,1024]{1,0:T(8,128)(2,1)} %get-tuple-element.42), channel_id=1, source_target_pairs={{0,1},{1,2},{2,3},{3,4},{4,5},{5,6},{6,7},{7,8},{8,9},{9,10},{10,1... | collective-permute-start | bytes 786440 | tf_op jit(solution)/shard_map/ppermute | solution.py:33
  7.7 1.3 collective-permute-start.1
  9.0 1.2 convert_reduce_fusion.1
  10.2 2.7 %convolution_convert_fusion.up_ref = bf16[256,1024]{1,0:T(8,128)(2,1)} fusion(bf16[256,1024]{1,0:T(8,128)(2,1)} %refs_2_.1, bf16[1024,1024]{1,0:T(8,128)(2,1)S(1)} %copy-done), kind=kOutput, calls=%fused_computation.41 | convolution fusion | flops 537133056 | bytes 3145728 | tf_op jit(solution)/shard_map/dot_general | solution.py:37
  12.9 0.6 pad_add_fusion.offset_ref
  13.5 1.1 collective-permute-done
  14.6 8.0 %collective-permute-done.1 = bf16[128,1024]{1,0:T(8,128)(2,1)S(1)} collective-permute-done((bf16[128,1024]{1,0:T(8,128)(2,1)S(1)}, bf16[128,1024]{1,0:T(8,128)(2,1)S(1)}, u32[]{:S(2)}, u32[]{:S(2)}) %collective-permute-start.1) | collective-permute-done | bytes 262176 | tf_op jit(solution)/shard_map/ppermute | solution.py:33
  22.9 0.4 fusion.2
  23.7 1.5 fusion.48.q_ref
  25.3 2.2 %fusion.26.v_ref = bf16[512,1024]{1,0:T(8,128)(2,1)} fusion(bf16[512,1024]{1,0:T(8,128)(2,1)S(1)} %fusion.4, bf16[3,1024,1024]{2,1,0:T(8,128)(2,1)S(1)} %copy-done.8), kind=kOutput, calls=%fused_computation.30 | convolution fusion | flops 1074266112 | bytes 4194304 | tf_op jit(solution)/shard_map/dot_general | solution.py:37
  27.5 2.2 %fusion.23.k_ref = bf16[512,1024]{1,0:T(8,128)(2,1)} fusion(bf16[512,1024]{1,0:T(8,128)(2,1)S(1)} %fusion.4, bf16[3,1024,1024]{2,1,0:T(8,128)(2,1)S(1)} %copy-done.8), kind=kOutput, calls=%fused_computation.29 | convolution fusion | flops 1074266112 | bytes 4194304 | tf_op jit(solution)/shard_map/dot_general | solution.py:37
  29.8 1.0 copy.10
  30.8 13.6 %attention.1 = (bf16[256,1024]{1,0:T(8,128)(2,1)}, bf16[256,1024]{1,0:T(8,128)(2,1)}, f32[2,256,1024]{2,1,0:T(8,128)}, bf16[2,256,1024]{2,1,0:T(8,128)(2,1)}) custom-call(s32[2]{0:T(128)} %pad_add_fusion.offset_ref, bf16[256,1024]{1,0:T(8,128)(2,1)} %fusion.48.q_ref, bf16[512,1024]{1,0:T(8,128)(2,1)} %fusion.23.k_ref, bf16[512,1024]{1,0:T(8,128)(2,1)} %fusion.26.v_ref, ...), custom_call_target="tpu_custom_call" | custom-call | tf_op jit(solution)/shard_map/attention/pallas_call | solution.py:95
  44.4 2.0 %copy.9 = bf16[1024,256]{1,0:T(8,128)(2,1)} copy(bf16[1024,256]{0,1:T(8,128)(2,1)} %bitcast.57) | data formatting | bytes 1048576 | tf_op jit(solution)/shard_map/transpose | solution.py:280
  46.4 2.3 %fusion.59 = (bf16[2,128,1024]{2,1,0:T(8,128)(2,1)}, bf16[2,128,1024]{2,1,0:T(8,128)(2,1)}) fusion(bf16[2,256,1024]{2,1,0:T(8,128)(2,1)} %get-tuple-element.35), kind=kLoop, calls=%fused_computation.66 | loop fusion | bytes 2097152 | tf_op jit(solution)/shard_map/slice | solution.py:277
  48.7 1.3 collective-permute-start.3
  50.0 5.3 %collective-permute-start.2 = (bf16[2,128,1024]{2,1,0:T(8,128)(2,1)}, bf16[2,128,1024]{2,1,0:T(8,128)(2,1)}, u32[]{:S(2)}, u32[]{:S(2)}) collective-permute-start(bf16[2,128,1024]{2,1,0:T(8,128)(2,1)} %get-tuple-element.41), channel_id=1, source_target_pairs={{0,1},{1,2},{2,3},{3,4},{4,5},{5,6},{6,7},{7,8},{8,9},{9,10},{10,1... | collective-permute-start | bytes 1572872 | tf_op jit(solution)/shard_map/ppermute | solution.py:33
  55.4 1.5 fusion.41
  56.9 44.7 %scatter_products_0.1 = f32[2,128,256]{2,1,0:T(8,128)} custom-call(bf16[8,128,256]{2,1,0:T(8,128)(2,1)} %bitcast.58, bf16[8,128,256]{2,1,0:T(8,128)(2,1)} %bitcast.54, bf16[256,1024]{1,0:T(8,128)(2,1)} %refs_2_.1, bf16[256,1024]{1,0:T(8,128)(2,1)} %get-tuple-element.33.refs_3_), custom_call_target="tpu_custom_call" | custom-call | flops 1073741824 | bytes 41943040 | tf_op jit(solution)/shard_map/scatter_products_0/pallas_call | solution.py:239
  101.5 1.6 slice_bitcast_fusion.1
  103.2 2.5 %add_dynamic-update-slice_fusion = f32[2,256,1024]{2,1,0:T(8,128)} fusion(f32[2,256,1024]{2,1,0:T(8,128)} %get-tuple-element.34, bf16[2,128,1024]{2,1,0:T(8,128)(2,1)} %collective-permute-done.2), kind=kLoop, calls=%fused_computation.50 | loop fusion | flops 524288 | bytes 2621440 | tf_op jit(solution)/shard_map/scatter-add | solution.py:282
  105.7 2.4 %fusion.53 = f32[2,256,1024]{2,1,0:T(8,128)} fusion(f32[2,256,1024]{2,1,0:T(8,128)} %add_dynamic-update-slice_fusion, bf16[2,128,1024]{2,1,0:T(8,128)(2,1)S(1)} %collective-permute-done.3), kind=kLoop, calls=%fused_computation.47 | loop fusion | flops 524288 | bytes 2621440 | tf_op jit(solution)/shard_map/scatter-add | solution.py:283
  108.1 2.5 %fusion.54 = (bf16[256,1024]{1,0:T(8,128)(2,1)}, bf16[256,1024]{1,0:T(8,128)(2,1)S(1)}) fusion(f32[2,256,1024]{2,1,0:T(8,128)} %fusion.53), kind=kLoop, calls=%fused_computation.51 | loop fusion | bytes 2097152 | tf_op jit(solution)/shard_map/convert_element_type | solution.py:284
  110.6 0.8 copy-done.5
  111.4 3.3 %fusion.5 = f32[256,1024]{1,0:T(8,128)} fusion(bf16[256,1024]{1,0:T(8,128)(2,1)S(1)} %get-tuple-element.39.refs_3_, bf16[3,1024,1024]{2,1,0:T(8,128)(2,1)} %param.12), kind=kOutput, calls=%fused_computation.7 | convolution fusion | flops 536870912 | bytes 3670016 | tf_op jit(solution)/shard_map/dot_general | solution.py:37
  114.7 46.3 %scatter_products_1.1 = f32[2,128,256]{2,1,0:T(8,128)} custom-call(bf16[8,128,256]{2,1,0:T(8,128)(2,1)} %bitcast.55, bf16[8,128,256]{2,1,0:T(8,128)(2,1)} %bitcast.56, bf16[256,1024]{1,0:T(8,128)(2,1)} %get-tuple-element.38.refs_2_, bf16[256,1024]{1,0:T(8,128)(2,1)} %copy-done.5), custom_call_target="tpu_custom_call" | custom-call | flops 1073741824 | bytes 41943040 | tf_op jit(solution)/shard_map/scatter_products_1/pallas_call | solution.py:239
  161.0 2.4 %fusion.9 = f32[256,1024]{1,0:T(8,128)S(1)} fusion(bf16[256,1024]{1,0:T(8,128)(2,1)S(1)} %copy-done.4, bf16[3,1024,1024]{2,1,0:T(8,128)(2,1)} %param.12), kind=kOutput, calls=%fused_computation.11 | convolution fusion | flops 536870912 | bytes 3670016 | tf_op jit(solution)/shard_map/dot_general | solution.py:37
  163.5 2.6 %fusion.51 = (f32[256]{0:T(256)S(1)}, f32[256]{0:T(256)S(1)}, f32[256,1024]{1,0:T(8,128)S(1)}) fusion(bf16[256,1024]{1,0:T(8,128)(2,1)S(1)} %copy-done.1, f32[256]{0:T(256)S(1)} %broadcast_multiply_fusion.1, f32[1024]{0:T(1024)S(1)} %copy-done.7, f32[256,1024]{1,0:T(8,128)S(1)} %copy-done.10, f32[256,1024]{1,0:T(8,128)S(1)} %fusion.9, ...), kind=kOutput, calls=%fused_computation.42 | convolution fusion | flops 539753984 | bytes 6298624 | tf_op jit(solution)/shard_map/dot_general | solution.py:37
  166.1 0.4 fusion.58
  166.5 1.2 add_convert_fusion
  167.7 0.8 pad_maximum_fusion.1
  (31 shorter events, 0.7 us)
Async XLA Ops:
  0.6 9.5 %copy-start = (bf16[1024,1024]{1,0:T(8,128)(2,1)S(1)}, bf16[1024,1024]{1,0:T(8,128)(2,1)}, u32[]{:S(2)}) copy-start(bf16[1024,1024]{1,0:T(8,128)(2,1)} %param.13) | copy-start | bytes 6291460
  2.6 20.1 %copy-start.1 = (bf16[256,1024]{1,0:T(8,128)(2,1)S(1)}, bf16[256,1024]{1,0:T(8,128)(2,1)}, u32[]{:S(2)}) copy-start(bf16[256,1024]{1,0:T(8,128)(2,1)} %param.9) | copy-start | bytes 1572868
  2.6 12.1 %collective-permute-start = (bf16[128,1024]{1,0:T(8,128)(2,1)}, bf16[128,1024]{1,0:T(8,128)(2,1)S(1)}, u32[]{:S(2)}, u32[]{:S(2)}) collective-permute-start(bf16[128,1024]{1,0:T(8,128)(2,1)} %get-tuple-element.42), channel_id=1, source_target_pairs={{0,1},{1,2},{2,3},{3,4},{4,5},{5,6},{6,7},{7,8},{8,9},{9,10},{10,1... | collective-permute-start | bytes 786440 | tf_op jit(solution)/shard_map/ppermute | solution.py:33
  7.7 15.0 %collective-permute-start.1 = (bf16[128,1024]{1,0:T(8,128)(2,1)S(1)}, bf16[128,1024]{1,0:T(8,128)(2,1)S(1)}, u32[]{:S(2)}, u32[]{:S(2)}) collective-permute-start(bf16[128,1024]{1,0:T(8,128)(2,1)S(1)} %get-tuple-element.43), channel_id=1, source_target_pairs={{1,0},{2,1},{3,2},{4,3},{5,4},{6,5},{7,6},{8,7},{9,8},{10,9},{11,1... | collective-permute-start | bytes 786440 | tf_op jit(solution)/shard_map/ppermute | solution.py:33
  10.2 13.1 %copy-start.7 = (f32[1024]{0:T(1024)S(1)}, f32[1024]{0:T(1024)}, u32[]{:S(2)}) copy-start(f32[1024]{0:T(1024)} %param.11) | copy-start | bytes 12292
  10.2 13.6 %copy-start.8 = (bf16[3,1024,1024]{2,1,0:T(8,128)(2,1)S(1)}, bf16[3,1024,1024]{2,1,0:T(8,128)(2,1)}, u32[]{:S(2)}) copy-start(bf16[3,1024,1024]{2,1,0:T(8,128)(2,1)} %param.12) | copy-start | bytes 18874372
  46.4 8.9 %copy-start.3 = (bf16[256,1024]{1,0:T(8,128)(2,1)S(1)}, bf16[256,1024]{1,0:T(8,128)(2,1)}, u32[]{:S(2)}) copy-start(bf16[256,1024]{1,0:T(8,128)(2,1)} %get-tuple-element.32) | copy-start | bytes 1572868
  48.7 57.0 %collective-permute-start.3 = (bf16[2,128,1024]{2,1,0:T(8,128)(2,1)}, bf16[2,128,1024]{2,1,0:T(8,128)(2,1)S(1)}, u32[]{:S(2)}, u32[]{:S(2)}) collective-permute-start(bf16[2,128,1024]{2,1,0:T(8,128)(2,1)} %get-tuple-element.40), channel_id=1, source_target_pairs={{1,0},{2,1},{3,2},{4,3},{5,4},{6,5},{7,6},{8,7},{9,8},{10,9},{11,1... | collective-permute-start | bytes 1572872 | tf_op jit(solution)/shard_map/ppermute | solution.py:33
  50.0 53.2 %collective-permute-start.2 = (bf16[2,128,1024]{2,1,0:T(8,128)(2,1)}, bf16[2,128,1024]{2,1,0:T(8,128)(2,1)}, u32[]{:S(2)}, u32[]{:S(2)}) collective-permute-start(bf16[2,128,1024]{2,1,0:T(8,128)(2,1)} %get-tuple-element.41), channel_id=1, source_target_pairs={{0,1},{1,2},{2,3},{3,4},{4,5},{5,6},{6,7},{7,8},{8,9},{9,10},{10,1... | collective-permute-start | bytes 1572872 | tf_op jit(solution)/shard_map/ppermute | solution.py:33
  110.6 0.8 copy-start.5
  114.7 46.3 %copy-start.4 = (bf16[256,1024]{1,0:T(8,128)(2,1)S(1)}, bf16[256,1024]{1,0:T(8,128)(2,1)}, u32[]{:S(2)}) copy-start(bf16[256,1024]{1,0:T(8,128)(2,1)} %get-tuple-element.38.refs_2_) | copy-start | bytes 1572868
  161.0 2.5 %copy-start.9 = (bf16[256,1024]{1,0:T(8,128)(2,1)S(1)}, bf16[256,1024]{1,0:T(8,128)(2,1)}, u32[]{:S(2)}) copy-start(bf16[256,1024]{1,0:T(8,128)(2,1)} %get-tuple-element.33.refs_3_) | copy-start | bytes 1572868
  161.0 2.5 %copy-start.10 = (f32[256,1024]{1,0:T(8,128)S(1)}, f32[256,1024]{1,0:T(8,128)}, u32[]{:S(2)}) copy-start(f32[256,1024]{1,0:T(8,128)} %fusion.5) | copy-start | bytes 3145732
  163.4 3.1 %copy-start.2 = (bf16[256,1024]{1,0:T(8,128)(2,1)S(1)}, bf16[256,1024]{1,0:T(8,128)(2,1)}, u32[]{:S(2)}) copy-start(bf16[256,1024]{1,0:T(8,128)(2,1)} %refs_2_.1) | copy-start | bytes 1572868
  166.1 1.6 copy-start.6

commit v2 on v0

v2 whole, which is shorter than its diff:
```python
import functools

import jax
import jax.numpy as jnp
from jax import lax
from jax.experimental import pallas as pl
from jax.experimental.pallas import tpu as pltpu
from jax.sharding import PartitionSpec as P

HEAD_SIZE = 128
WINDOW = 128

EPSILON = 1e-05
MASKED = -1e30
AXES = ("seq", "head")


def dot(a, b, contract):
    return lax.dot_general(a, b, (contract, ((), ())), preferred_element_type=jnp.float32)


def bits_of(size):
    return list(range(size.bit_length() - 1))


def block_kernel(
    sizes, orders, scale,
    frames, cotangent, gain, w_qkv_hbm, w_out_hbm,
    output, grad_frames, grad_qkv, grad_out,
    w_qkv, w_out, normed, normed_t, query, key, value, upstream, attended, attended_t,
    grad_query, mid, edge_out, edge_in, grad_pair, grad_normed, held, landed, halo,
    weight_sem, halo_send, halo_recv, edge_send, edge_recv, send_sem, recv_sem,
):
    seq_size, head_size = sizes
    devices = tiles = seq_size * head_size
    length, channels = frames.shape
    chunks, stages = len(orders), len(orders[0])
    tile_rows, tile_cols = held.shape[2:]
    place = {axis: lax.axis_index(axis) for axis in AXES}
    position = place["seq"] * head_size + place["head"]
    bf16, f32 = jnp.bfloat16, jnp.float32
    strip = min(256, channels)

    def neighbour(step):
        there = (position + step + devices) % devices
        return (there // head_size, there % head_size)

    def bit_at(order):
        axis, bit = order
        return (place[axis] // 2**bit) % 2

    def partner(order):
        axis, bit = order
        moved = place[axis] + (1 - 2 * bit_at(order)) * 2**bit
        return tuple(moved if name == axis else place[name] for name in AXES)

    weights = [pltpu.make_async_copy(w_out_hbm, w_out, weight_sem.at[3])]
    for which in range(3):
        weights.append(
            pltpu.make_async_copy(w_qkv_hbm.at[which], w_qkv.at[which], weight_sem.at[which])
        )
    for one in weights:
        one.start()

    greeted = [partner(order) for order in orders[0]] + [neighbour(1), neighbour(-1)]
    barrier = pltpu.get_barrier_semaphore()
    for device in greeted:
        pl.semaphore_signal(barrier, inc=1, device_id=device, device_id_type=pl.DeviceIdType.MESH)
    pl.semaphore_wait(barrier, len(greeted))

    def halo_copy(side):
        rows = pl.ds(length - WINDOW, WINDOW) if side == 0 else pl.ds(0, WINDOW)
        return pltpu.make_async_remote_copy(
            src_ref=frames.at[rows],
            dst_ref=halo.at[side],
            send_sem=halo_send.at[side],
            recv_sem=halo_recv.at[side],
            device_id=neighbour(1 if side == 0 else -1),
            device_id_type=pl.DeviceIdType.MESH,
        )

    halo_copy(0).start()
    halo_copy(1).start()

    def standardise(values):
        average = jnp.mean(values, axis=-1, keepdims=True)
        centered = values - average
        variance = jnp.mean(centered * centered, axis=-1, keepdims=True)
        inverse = lax.rsqrt(variance + EPSILON)
        return centered * inverse, inverse

    few = 64

    def norm_rows(source, target_row, rows):
        def one(step, carry):
            values = source[pl.ds(pl.multiple_of(step * few, few), few), :].astype(f32)
            rounded = (standardise(values)[0] * gain[...]).astype(bf16)
            normed[pl.ds(pl.multiple_of(target_row + step * few, few), few), :] = rounded
            return carry

        lax.fori_loop(0, rows // few, one, 0)

    def multiply_into(target, rows, left, weight, side):
        for start in range(0, channels, strip):
            cols = slice(start, start + strip)
            other = weight[:, cols] if side == 0 else weight[cols, :]
            target[rows, cols] = dot(left, other, ((1,), (side,))).astype(target.dtype)

    norm_rows(frames, WINDOW, length)
    own = slice(WINDOW, WINDOW + length)
    for start in range(0, length, 128):
        for col in range(0, channels, 128):
            tile = normed[WINDOW + start : WINDOW + start + 128, col : col + 128]
            normed_t[col : col + 128, start : start + 128] = tile.astype(f32).T.astype(bf16)
    weights[0].wait()
    everything = slice(0, length)
    multiply_into(upstream, everything, cotangent[...], w_out, 1)
    for which, target, rows in ((0, query, everything), (1, key, own), (2, value, own)):
        weights[1 + which].wait()
        multiply_into(target, rows, normed[own, :], w_qkv.at[which], 0)
    for side in range(2):
        halo_copy(side).wait()
        start = side * (length + WINDOW)
        norm_rows(halo.at[side], start, WINDOW)
    for side in range(2):
        start = side * (length + WINDOW)
        rows = slice(start, start + WINDOW)
        multiply_into(key, rows, normed[rows, :], w_qkv.at[1], 0)
        multiply_into(value, rows, normed[rows, :], w_qkv.at[2], 0)

    pairs, wide = edge_out.shape[0], edge_out.shape[-1]

    def edge_copy(pair, side):
        return pltpu.make_async_remote_copy(
            src_ref=edge_out.at[pair, side],
            dst_ref=edge_in.at[pair, side],
            send_sem=edge_send.at[pair, side],
            recv_sem=edge_recv.at[pair, side],
            device_id=neighbour(-1 if side == 0 else 1),
            device_id_type=pl.DeviceIdType.MESH,
        )

    blocks = length // WINDOW
    span = 3 * WINDOW
    score_scale = HEAD_SIZE ** (-0.5)
    row = lax.broadcasted_iota(jnp.int32, (WINDOW, span), 0)
    col = lax.broadcasted_iota(jnp.int32, (WINDOW, span), 1)
    near = (col >= row) & (col <= row + 2 * WINDOW)

    def attend(pair, carry):
        for head in range(wide // HEAD_SIZE):
            lane = pl.multiple_of(pair * wide + head * HEAD_SIZE, HEAD_SIZE)
            lanes = pl.ds(lane, HEAD_SIZE)
            here = slice(head * HEAD_SIZE, (head + 1) * HEAD_SIZE)
            key_grads = [None] * (blocks + 2)
            value_grads = [None] * (blocks + 2)
            for block in range(blocks):
                rows = slice(block * WINDOW, (block + 1) * WINDOW)
                keys = slice(block * WINDOW, block * WINDOW + span)
                q, k, v, up = query[rows, lanes], key[keys, lanes], value[keys, lanes], upstream[rows, lanes]
                frame = position * length + (block - 1) * WINDOW + col
                allowed = near & (frame >= 0) & (frame < devices * length)
                scores = jnp.where(allowed, dot(q, k, ((1,), (1,))) * score_scale, MASKED)
                share = jnp.exp(scores - jnp.max(scores, axis=-1, keepdims=True))
                share = share * (1.0 / jnp.sum(share, axis=-1, keepdims=True))
                rounded = share.astype(bf16)
                mixed = dot(rounded, v, ((1,), (0,)))
                attended[rows, lanes] = mixed.astype(bf16)
                attended_t[lanes, rows] = mixed.T.astype(bf16)
                grad = dot(up, v, ((1,), (1,)))
                centre = jnp.sum(share * grad, axis=-1, keepdims=True)
                grad = (share * (grad - centre) * score_scale).astype(bf16)
                grad_query[rows, lanes] = dot(grad, k, ((1,), (0,))).astype(bf16)
                key_grad = dot(grad, q, ((0,), (0,)))
                value_grad = dot(rounded, up, ((0,), (0,)))
                for part in range(3):
                    piece = slice(part * WINDOW, (part + 1) * WINDOW)
                    for sums, term in ((key_grads, key_grad[piece]), (value_grads, value_grad[piece])):
                        before = sums[block + part]
                        sums[block + part] = term if before is None else before + term
            for which, sums in enumerate((key_grads, value_grads)):
                edge_out[pair, 0, which, :, here] = sums[0].astype(bf16)
                edge_out[pair, 1, which, :, here] = sums[-1].astype(bf16)
                for block in range(blocks):
                    rows = slice(block * WINDOW, (block + 1) * WINDOW)
                    mid[which, rows, lanes] = sums[block + 1]
        edge_copy(pair, 0).start()
        edge_copy(pair, 1).start()
        return carry

    lax.fori_loop(0, pairs, attend, 0)

    def base(chunk, stage):
        total = 0
        for step in range(stage):
            total = total + bit_at(orders[chunk][step]) * (tiles >> (step + 1))
        return total

    def landing(stage):
        return tiles - (tiles >> stage)

    def copy(chunk, stage):
        half = tiles >> (stage + 1)
        order = orders[chunk][stage]
        other = base(chunk, stage) + (1 - bit_at(order)) * half
        return pltpu.make_async_remote_copy(
            src_ref=held.at[chunk, pl.ds(other, half)],
            dst_ref=landed.at[chunk, pl.ds(landing(stage), half)],
            send_sem=send_sem.at[chunk, stage],
            recv_sem=recv_sem.at[chunk, stage],
            device_id=partner(order),
            device_id_type=pl.DeviceIdType.MESH,
        )

    def advance(chunk, stage):
        copy(chunk, stage).wait()
        half = tiles >> (stage + 1)
        keep = base(chunk, stage + 1)
        if stage == stages - 1:
            total = held[chunk, keep].astype(f32) + landed[chunk, landing(stage)].astype(f32)
            if chunk == 0:
                grad_out[...] = total * scale
            else:
                grad_qkv[chunk - 1] = total * scale
            return

        def add(step, carry):
            total = held[chunk, keep + step].astype(f32) + landed[chunk, landing(stage) + step].astype(f32)
            held[chunk, keep + step] = total.astype(bf16)
            return carry

        lax.fori_loop(0, half, add, 0)
        copy(chunk, stage + 1).start()

    def tile_place(chunk, axis, index):
        total = 0
        for step, (name, bit) in enumerate(orders[chunk]):
            if name == axis:
                total = total + ((index // 2**bit) % 2) * (tiles >> (step + 1))
        return total

    def products(chunk, left, right, half):
        def one(step, carry):
            block = 2 * step + half
            rows = pl.ds(pl.multiple_of(block * tile_rows, tile_rows), tile_rows)
            product = dot(left[rows, :], right[...], ((1,), (0,))).astype(bf16)
            down = tile_place(chunk, "seq", block)
            for col in range(head_size):
                held[chunk, down + tile_place(chunk, "head", col)] = product[
                    :, col * tile_cols : (col + 1) * tile_cols
                ]
            return carry

        lax.fori_loop(0, seq_size // 2, one, 0)

    def launch(chunk, left, right):
        mine = bit_at(orders[chunk][0])
        products(chunk, left, right, 1 - mine)
        copy(chunk, 0).start()
        products(chunk, left, right, mine)

    launch(0, attended_t, cotangent)
    launch(1, normed_t, grad_query)
    advance(0, 0)
    advance(1, 0)
    for start in range(0, channels, strip):
        cols = slice(start, start + strip)
        mixed = dot(attended[...], w_out[:, cols], ((1,), (0,)))
        output[:, cols] = (frames[:, cols].astype(f32) + mixed).astype(bf16)
    multiply_into(grad_normed, everything, grad_query[...], w_qkv.at[0], 1)

    def combine(pair, carry):
        edge_copy(pair, 0).wait()
        edge_copy(pair, 1).wait()
        lanes = pl.ds(pl.multiple_of(pair * wide, wide), wide)
        last = length - WINDOW
        for which in range(2):
            first_rows = mid[which, :WINDOW, lanes] + edge_in[pair, 1, which].astype(f32)
            grad_pair[which, :WINDOW, lanes] = first_rows.astype(bf16)
            last_rows = mid[which, last:, lanes] + edge_in[pair, 0, which].astype(f32)
            grad_pair[which, last:, lanes] = last_rows.astype(bf16)
            if last > WINDOW:
                grad_pair[which, WINDOW:last, lanes] = mid[which, WINDOW:last, lanes].astype(bf16)
        return carry

    lax.fori_loop(0, pairs, combine, 0)
    launch(2, normed_t, grad_pair.at[0])
    launch(3, normed_t, grad_pair.at[1])
    advance(0, 1)
    advance(1, 1)
    advance(2, 0)
    advance(3, 0)
    for start in range(0, channels, strip):
        cols = slice(start, start + strip)
        more = dot(grad_pair[0], w_qkv[1, cols, :], ((1,), (1,)))
        more = more + dot(grad_pair[1], w_qkv[2, cols, :], ((1,), (1,)))
        grad_normed[:, cols] += more
    for stage in range(2, stages):
        advance(0, stage)
        advance(1, stage)
        if stage == 2:

            def norm_back(step, carry):
                rows = pl.ds(pl.multiple_of(step * few, few), few)
                unit, inverse = standardise(frames[rows, :].astype(f32))
                grad = grad_normed[rows, :].astype(bf16).astype(f32) * gain[...]
                average = jnp.mean(grad, axis=-1, keepdims=True)
                along = jnp.mean(grad * unit, axis=-1, keepdims=True)
                grad = inverse * (grad - average - unit * along)
                grad_frames[rows, :] = (cotangent[rows, :].astype(f32) + grad).astype(bf16)
                return carry

            lax.fori_loop(0, length // few, norm_back, 0)
        advance(2, stage - 1)
        advance(3, stage - 1)
    advance(2, stages - 1)
    advance(3, stages - 1)


def shards(frames, cotangent, norm_gain, w_qkv, w_out):
    length, channels = frames.shape
    seq_size, head_size = lax.axis_size("seq"), lax.axis_size("head")
    devices = seq_size * head_size
    bordered = length + 2 * WINDOW
    wide = 2 * HEAD_SIZE
    pairs = channels // wide
    tile_rows, tile_cols = channels // seq_size, channels // head_size
    outer = [("seq", bit) for bit in bits_of(seq_size)[1:]]
    along = [("head", bit) for bit in bits_of(head_size)]
    first = [("seq", 0)]
    orders = [
        first + outer + along,
        first + outer[::-1] + along,
        first + along[:1] + outer + along[1:],
        first + along[:1] + outer[::-1] + along[1:],
    ]
    chunks, stages = len(orders), len(orders[0])
    bf16, f32 = jnp.bfloat16, jnp.float32
    vmem, anywhere = pl.BlockSpec(memory_space=pltpu.VMEM), pl.BlockSpec(memory_space=pl.ANY)
    dma = pltpu.SemaphoreType.DMA
    output, grad_frames, grad_qkv, grad_out = pl.pallas_call(
        functools.partial(block_kernel, (seq_size, head_size), orders, (devices * length) ** (-0.5)),
        out_shape=[
            jax.ShapeDtypeStruct((length, channels), bf16),
            jax.ShapeDtypeStruct((length, channels), bf16),
            jax.ShapeDtypeStruct((3, tile_rows, tile_cols), f32),
            jax.ShapeDtypeStruct((tile_rows, tile_cols), f32),
        ],
        in_specs=[vmem, vmem, vmem, anywhere, anywhere],
        out_specs=[vmem] * 4,
        scratch_shapes=[
            pltpu.VMEM((3, channels, channels), bf16),
            pltpu.VMEM((channels, channels), bf16),
            pltpu.VMEM((bordered, channels), bf16),
            pltpu.VMEM((channels, length), bf16),
            pltpu.VMEM((length, channels), bf16),
            pltpu.VMEM((bordered, channels), bf16),
            pltpu.VMEM((bordered, channels), bf16),
            pltpu.VMEM((length, channels), bf16),
            pltpu.VMEM((length, channels), bf16),
            pltpu.VMEM((channels, length), bf16),
            pltpu.VMEM((length, channels), bf16),
            pltpu.VMEM((2, length, channels), f32),
            pltpu.VMEM((pairs, 2, 2, WINDOW, wide), bf16),
            pltpu.VMEM((pairs, 2, 2, WINDOW, wide), bf16),
            pltpu.VMEM((2, length, channels), bf16),
            pltpu.VMEM((length, channels), f32),
            pltpu.VMEM((chunks, devices, tile_rows, tile_cols), bf16),
            pltpu.VMEM((chunks, devices, tile_rows, tile_cols), bf16),
            pltpu.VMEM((2, WINDOW, channels), bf16),
            dma((4,)),
            dma((2,)),
            dma((2,)),
            dma((pairs, 2)),
            dma((pairs, 2)),
            dma((chunks, stages)),
            dma((chunks, stages)),
        ],
        compiler_params=pltpu.CompilerParams(
            collective_id=0, has_side_effects=True, vmem_limit_bytes=60 * 2**20
        ),
        name="block",
    )(frames, cotangent, norm_gain.reshape(1, channels), w_qkv, w_out)
    return (output, grad_frames, grad_qkv, grad_out)


def solution(mesh):
    in_specs = (P(("seq", "head"), None), P(("seq", "head"), None), P(), P(), P())
    out_specs = (
        P(("seq", "head"), None),
        P(("seq", "head"), None),
        P(None, "seq", "head"),
        P("seq", "head"),
    )
    return jax.shard_map(shards, mesh=mesh, in_specs=in_specs, out_specs=out_specs, check_vma=False)
```

time: 553 us -> 106 us (0.19); the launches traced: 545 us -> 106 us
  waiting for transfers between devices: 220 us -> 0 us
  Pallas kernels: 0 us -> 98.1 us
  local copies, waits for them, and re-layouts: 90.1 us -> 7.07 us
  blocking collectives: 74.3 us -> 0 us
  matrix products: 68.8 us -> 0 us
  other arithmetic: 37.8 us -> 0 us
  starting transfers between devices: 24 us -> 0 us
  loops' own time: 15.4 us -> 0 us
  between operations: 14.6 us -> 0.64 us
    reduce_scatter x3 -> x0, waiting for transfers between devices: 132 us -> none  [the longest x2 110 us: sum_columns(): lax.psum_scatter(term.astype(jnp.bfloat16), 'head', scatter_dimension=2,...]
    pallas_call x0 -> x1, Pallas kernels: none -> 98.1 us  [shards(): pl.pallas_call(functools.partial(block_kernel, (seq_size, head_size), ord...]
    all_to_all x1 -> x0, blocking collectives: 74.3 us -> none  [to_time(): lax.all_to_all(stacked, 'head', split_axis=1, concat_axis=2, tiled=True)]
    dot_general x20 -> x0, matrix products: 68.8 us -> none  [the longest x8 23.7 us: one_block(): jnp.einsum('qhe,khe->hqk', query_part, key_part, precision=lax.Precision....]
    all_to_all x3 -> x0, waiting for transfers between devices: 47 us -> none  [the longest x2 47 us: to_heads(): lax.all_to_all(stacked, 'head', split_axis=2, concat_axis=1, tiled=True)]
    unnamed x5 -> x0, waiting for transfers between devices: 40.8 us -> none
    dynamic_slice x18 -> x0, local copies, waits for them, and re-layouts: 18 us -> none  [the longest x4 7.11 us: one_block(): lax.dynamic_slice_in_dim(key_rows, anchor, key_span, 0)]
    another operation x2 -> x0, loops' own time: 15.4 us -> none  [attention(): lax.map(jax.checkpoint(one_block), jnp.arange(block_count, dtype=jnp.int32))]
  transfers between devices with their start and end apart: 11 -> 0, of which waited for: 6 -> 0; matrix products, arithmetic and copies ran while one was open for 22% -> 0% of each run, Pallas kernels for 0% -> 0%
where the time goes in v2:
time: 106 us
  Pallas kernels  98.1 us (93%)
  local copies, waits for them, and re-layouts  7.07 us (7%)
    pallas_call x1, Pallas kernels, shards(): pl.pallas_call(functools.partial(block_kernel, (seq_size, head_size), ord...  98.1 us
    unnamed x4, local copies, waits for them, and re-layouts  7.07 us

profile of v2, /device:TPU:0, one launch (start us, length us, event | category | flops | bytes accessed | tf_op | source)
XLA Modules:
  0.0 105.8 jit_solution(1263095153838978194)
XLA Ops:
  0.6 98.1 %block.1 = (bf16[256,1024]{1,0:T(8,128)(2,1)}, bf16[256,1024]{1,0:T(8,128)(2,1)}, f32[3,128,256]{2,1,0:T(8,128)}, f32[128,256]{1,0:T(8,128)}) custom-call(bf16[256,1024]{1,0:T(8,128)(2,1)} %frames.1, bf16[256,1024]{1,0:T(8,128)(2,1)} %cotangent.1, f32[1,1024]{1,0:T(1,128)} %bitcast.1, bf16[3,1024,1024]{2,1,0:T(8,128)(2,1)} %w_qkv_hbm.1, ...), custom_call_target="tpu_custom_call" | custom-call | tf_op jit(solution)/shard_map/block/pallas_call | solution.py:341
  98.8 1.9 %copy.13 = bf16[256,1024]{1,0:T(8,128)(2,1)} copy(bf16[256,1024]{1,0:T(8,128)(2,1)} %get-tuple-element.8) | data formatting | bytes 1048576
  100.6 1.9 %copy.14 = bf16[256,1024]{1,0:T(8,128)(2,1)} copy(bf16[256,1024]{1,0:T(8,128)(2,1)} %get-tuple-element.9) | data formatting | bytes 1048576
  102.5 1.8 %copy.15 = f32[3,128,256]{2,1,0:T(8,128)} copy(f32[3,128,256]{2,1,0:T(8,128)} %get-tuple-element.10) | data formatting | bytes 786432
  104.3 1.6 %copy.16 = f32[128,256]{1,0:T(8,128)} copy(f32[128,256]{1,0:T(8,128)} %get-tuple-element.11) | data formatting | bytes 262144

commit v3 on v2

--- a/solution.py
+++ b/solution.py
@@ -24,11 +24,11 @@
 
 
 def block_kernel(
-    sizes, orders, scale,
+    sizes, orders,
     frames, cotangent, gain, w_qkv_hbm, w_out_hbm,
     output, grad_frames, grad_qkv, grad_out,
     w_qkv, w_out, normed, normed_t, query, key, value, upstream, attended, attended_t,
-    grad_query, mid, edge_out, edge_in, grad_pair, grad_normed, held, landed, halo,
+    grad_query, grad_pair, shares, edge_out, edge_in, grad_normed, held, landed, halo,
     weight_sem, halo_send, halo_recv, edge_send, edge_recv, send_sem, recv_sem,
 ):
     seq_size, head_size = sizes
@@ -108,10 +108,14 @@
 
     norm_rows(frames, WINDOW, length)
     own = slice(WINDOW, WINDOW + length)
-    for start in range(0, length, 128):
-        for col in range(0, channels, 128):
-            tile = normed[WINDOW + start : WINDOW + start + 128, col : col + 128]
-            normed_t[col : col + 128, start : start + 128] = tile.astype(f32).T.astype(bf16)
+
+    def turn(first, last):
+        for start in range(first, last, 128):
+            for col in range(0, channels, 128):
+                tile = normed[start : start + 128, col : col + 128]
+                normed_t[col : col + 128, start : start + 128] = tile.astype(f32).T.astype(bf16)
+
+    turn(WINDOW, WINDOW + length)
     weights[0].wait()
     everything = slice(0, length)
     multiply_into(upstream, everything, cotangent[...], w_out, 1)
@@ -128,14 +132,15 @@
         multiply_into(key, rows, normed[rows, :], w_qkv.at[1], 0)
         multiply_into(value, rows, normed[rows, :], w_qkv.at[2], 0)
 
-    pairs, wide = edge_out.shape[0], edge_out.shape[-1]
-
-    def edge_copy(pair, side):
+    wide = 2 * HEAD_SIZE
+    pairs = channels // wide
+
+    def edge_copy(side):
         return pltpu.make_async_remote_copy(
-            src_ref=edge_out.at[pair, side],
-            dst_ref=edge_in.at[pair, side],
-            send_sem=edge_send.at[pair, side],
-            recv_sem=edge_recv.at[pair, side],
+            src_ref=edge_out.at[side],
+            dst_ref=edge_in.at[side],
+            send_sem=edge_send.at[side],
+            recv_sem=edge_recv.at[side],
             device_id=neighbour(-1 if side == 0 else 1),
             device_id_type=pl.DeviceIdType.MESH,
         )
@@ -147,26 +152,37 @@
     col = lax.broadcasted_iota(jnp.int32, (WINDOW, span), 1)
     near = (col >= row) & (col <= row + 2 * WINDOW)
 
-    def attend(pair, carry):
+    def forward(pair, carry):
         for head in range(wide // HEAD_SIZE):
             lane = pl.multiple_of(pair * wide + head * HEAD_SIZE, HEAD_SIZE)
             lanes = pl.ds(lane, HEAD_SIZE)
-            here = slice(head * HEAD_SIZE, (head + 1) * HEAD_SIZE)
+            for block in range(blocks):
+                rows = slice(block * WINDOW, (block + 1) * WINDOW)
+                keys = slice(block * WINDOW, block * WINDOW + span)
+                q, k, v = query[rows, lanes], key[keys, lanes], value[keys, lanes]
+                frame = position * length + (block - 1) * WINDOW + col
+                allowed = near & (frame >= 0) & (frame < devices * length)
+                scores = jnp.where(allowed, dot(q, k, ((1,), (1,))) * score_scale, MASKED)
+                share = jnp.exp(scores - jnp.max(scores, axis=-1, keepdims=True))
+                share = (share * (1.0 / jnp.sum(share, axis=-1, keepdims=True))).astype(bf16)
+                shares[pair * (wide // HEAD_SIZE) + head, block] = share
+                mixed = dot(share, v, ((1,), (0,)))
+                attended[rows, lanes] = mixed.astype(bf16)
+                attended_t[lanes, rows] = mixed.T.astype(bf16)
+        return carry
+
+    def backward(pair, carry):
+        for head in range(wide // HEAD_SIZE):
+            lane = pl.multiple_of(pair * wide + head * HEAD_SIZE, HEAD_SIZE)
+            lanes = pl.ds(lane, HEAD_SIZE)
             key_grads = [None] * (blocks + 2)
             value_grads = [None] * (blocks + 2)
             for block in range(blocks):
                 rows = slice(block * WINDOW, (block + 1) * WINDOW)
                 keys = slice(block * WINDOW, block * WINDOW + span)
                 q, k, v, up = query[rows, lanes], key[keys, lanes], value[keys, lanes], upstream[rows, lanes]
-                frame = position * length + (block - 1) * WINDOW + col
-                allowed = near & (frame >= 0) & (frame < devices * length)
-                scores = jnp.where(allowed, dot(q, k, ((1,), (1,))) * score_scale, MASKED)
-                share = jnp.exp(scores - jnp.max(scores, axis=-1, keepdims=True))
-                share = share * (1.0 / jnp.sum(share, axis=-1, keepdims=True))
-                rounded = share.astype(bf16)
-                mixed = dot(rounded, v, ((1,), (0,)))
-                attended[rows, lanes] = mixed.astype(bf16)
-                attended_t[lanes, rows] = mixed.T.astype(bf16)
+                rounded = shares[pair * (wide // HEAD_SIZE) + head, block]
+                share = rounded.astype(f32)
                 grad = dot(up, v, ((1,), (1,)))
                 centre = jnp.sum(share * grad, axis=-1, keepdims=True)
                 grad = (share * (grad - centre) * score_scale).astype(bf16)
@@ -179,16 +195,10 @@
                         before = sums[block + part]
                         sums[block + part] = term if before is None else before + term
             for which, sums in enumerate((key_grads, value_grads)):
-                edge_out[pair, 0, which, :, here] = sums[0].astype(bf16)
-                edge_out[pair, 1, which, :, here] = sums[-1].astype(bf16)
-                for block in range(blocks):
+                for block in range(blocks + 2):
                     rows = slice(block * WINDOW, (block + 1) * WINDOW)
-                    mid[which, rows, lanes] = sums[block + 1]
-        edge_copy(pair, 0).start()
-        edge_copy(pair, 1).start()
+                    grad_pair[which, rows, lanes] = sums[block].astype(bf16)
         return carry
-
-    lax.fori_loop(0, pairs, attend, 0)
 
     def base(chunk, stage):
         total = 0
@@ -219,9 +229,9 @@
         if stage == stages - 1:
             total = held[chunk, keep].astype(f32) + landed[chunk, landing(stage)].astype(f32)
             if chunk == 0:
-                grad_out[...] = total * scale
+                grad_out[...] = total
             else:
-                grad_qkv[chunk - 1] = total * scale
+                grad_qkv[chunk - 1] = total
             return
 
         def add(step, carry):
@@ -239,11 +249,11 @@
                 total = total + ((index // 2**bit) % 2) * (tiles >> (step + 1))
         return total
 
-    def products(chunk, left, right, half):
+    def products(chunk, left, right, depth, half):
         def one(step, carry):
             block = 2 * step + half
             rows = pl.ds(pl.multiple_of(block * tile_rows, tile_rows), tile_rows)
-            product = dot(left[rows, :], right[...], ((1,), (0,))).astype(bf16)
+            product = dot(left[rows, depth], right[...], ((1,), (0,))).astype(bf16)
             down = tile_place(chunk, "seq", block)
             for col in range(head_size):
                 held[chunk, down + tile_place(chunk, "head", col)] = product[
@@ -253,68 +263,74 @@
 
         lax.fori_loop(0, seq_size // 2, one, 0)
 
-    def launch(chunk, left, right):
+    def launch(chunk, left, right, depth):
         mine = bit_at(orders[chunk][0])
-        products(chunk, left, right, 1 - mine)
+        products(chunk, left, right, depth, 1 - mine)
         copy(chunk, 0).start()
-        products(chunk, left, right, mine)
-
-    launch(0, attended_t, cotangent)
-    launch(1, normed_t, grad_query)
+        products(chunk, left, right, depth, mine)
+
+    lax.fori_loop(0, pairs, forward, 0)
+    launch(0, attended_t, cotangent, everything)
+    lax.fori_loop(0, pairs // 2, backward, 0)
     advance(0, 0)
+    lax.fori_loop(pairs // 2, pairs, backward, 0)
+    launch(1, normed_t, grad_query, own)
+    turn(0, WINDOW)
+    turn(WINDOW + length, 2 * WINDOW + length)
+    launch(2, normed_t, grad_pair.at[0], slice(0, 2 * WINDOW + length))
     advance(1, 0)
+    launch(3, normed_t, grad_pair.at[1], slice(0, 2 * WINDOW + length))
+    advance(2, 0)
+
+    def pair_back(rows, cols):
+        term = dot(grad_pair[0, rows, :], w_qkv[1, cols, :], ((1,), (1,)))
+        return term + dot(grad_pair[1, rows, :], w_qkv[2, cols, :], ((1,), (1,)))
+
+    for side in range(2):
+        start = side * (length + WINDOW)
+        for strip_start in range(0, channels, strip):
+            cols = slice(strip_start, strip_start + strip)
+            edge_out[side, :, cols] = pair_back(slice(start, start + WINDOW), cols).astype(bf16)
+        edge_copy(side).start()
+    advance(3, 0)
     for start in range(0, channels, strip):
         cols = slice(start, start + strip)
         mixed = dot(attended[...], w_out[:, cols], ((1,), (0,)))
         output[:, cols] = (frames[:, cols].astype(f32) + mixed).astype(bf16)
-    multiply_into(grad_normed, everything, grad_query[...], w_qkv.at[0], 1)
-
-    def combine(pair, carry):
-        edge_copy(pair, 0).wait()
-        edge_copy(pair, 1).wait()
-        lanes = pl.ds(pl.multiple_of(pair * wide, wide), wide)
-        last = length - WINDOW
-        for which in range(2):
-            first_rows = mid[which, :WINDOW, lanes] + edge_in[pair, 1, which].astype(f32)
-            grad_pair[which, :WINDOW, lanes] = first_rows.astype(bf16)
-            last_rows = mid[which, last:, lanes] + edge_in[pair, 0, which].astype(f32)
-            grad_pair[which, last:, lanes] = last_rows.astype(bf16)
-            if last > WINDOW:
-                grad_pair[which, WINDOW:last, lanes] = mid[which, WINDOW:last, lanes].astype(bf16)
-        return carry
-
-    lax.fori_loop(0, pairs, combine, 0)
-    launch(2, normed_t, grad_pair.at[0])
-    launch(3, normed_t, grad_pair.at[1])
     advance(0, 1)
-    advance(1, 1)
-    advance(2, 0)
-    advance(3, 0)
     for start in range(0, channels, strip):
         cols = slice(start, start + strip)
-        more = dot(grad_pair[0], w_qkv[1, cols, :], ((1,), (1,)))
-        more = more + dot(grad_pair[1], w_qkv[2, cols, :], ((1,), (1,)))
-        grad_normed[:, cols] += more
+        grad_normed[:, cols] = pair_back(own, cols) + dot(grad_query[...], w_qkv[0, cols, :], ((1,), (1,)))
+    advance(1, 1)
+    advance(2, 1)
+    advance(3, 1)
+
+    def norm_back(step, carry):
+        rows = pl.ds(pl.multiple_of(step * few, few), few)
+        unit, inverse = standardise(frames[rows, :].astype(f32))
+        grad = grad_normed[rows, :].astype(bf16).astype(f32) * gain[...]
+        average = jnp.mean(grad, axis=-1, keepdims=True)
+        along = jnp.mean(grad * unit, axis=-1, keepdims=True)
+        grad = inverse * (grad - average - unit * along)
+        grad_frames[rows, :] = (cotangent[rows, :].astype(f32) + grad).astype(bf16)
+        return carry
+
     for stage in range(2, stages):
-        advance(0, stage)
-        advance(1, stage)
+        for chunk in range(chunks):
+            advance(chunk, stage)
         if stage == 2:
-
-            def norm_back(step, carry):
-                rows = pl.ds(pl.multiple_of(step * few, few), few)
-                unit, inverse = standardise(frames[rows, :].astype(f32))
-                grad = grad_normed[rows, :].astype(bf16).astype(f32) * gain[...]
-                average = jnp.mean(grad, axis=-1, keepdims=True)
-                along = jnp.mean(grad * unit, axis=-1, keepdims=True)
-                grad = inverse * (grad - average - unit * along)
-                grad_frames[rows, :] = (cotangent[rows, :].astype(f32) + grad).astype(bf16)
-                return carry
-
+            edge_copy(0).wait()
+            edge_copy(1).wait()
+            grad_normed[:WINDOW, :] += edge_in[1].astype(f32)
+            grad_normed[length - WINDOW :, :] += edge_in[0].astype(f32)
             lax.fori_loop(0, length // few, norm_back, 0)
-        advance(2, stage - 1)
-        advance(3, stage - 1)
-    advance(2, stages - 1)
-    advance(3, stages - 1)
+
+
+def deliver_kernel(scale, output, grad_frames, grad_qkv, grad_out, *targets):
+    targets[0][...] = output[...]
+    targets[1][...] = grad_frames[...]
+    targets[2][...] = grad_qkv[...] * scale
+    targets[3][...] = grad_out[...] * scale
 
 
 def shards(frames, cotangent, norm_gain, w_qkv, w_out):
@@ -322,8 +338,6 @@
     seq_size, head_size = lax.axis_size("seq"), lax.axis_size("head")
     devices = seq_size * head_size
     bordered = length + 2 * WINDOW
-    wide = 2 * HEAD_SIZE
-    pairs = channels // wide
     tile_rows, tile_cols = channels // seq_size, channels // head_size
     outer = [("seq", bit) for bit in bits_of(seq_size)[1:]]
     along = [("head", bit) for bit in bits_of(head_size)]
@@ -331,28 +345,29 @@
     orders = [
         first + outer + along,
         first + outer[::-1] + along,
-        first + along[:1] + outer + along[1:],
         first + along[:1] + outer[::-1] + along[1:],
+        first + outer[:1] + along[:1] + outer[1:] + along[1:],
     ]
     chunks, stages = len(orders), len(orders[0])
     bf16, f32 = jnp.bfloat16, jnp.float32
     vmem, anywhere = pl.BlockSpec(memory_space=pltpu.VMEM), pl.BlockSpec(memory_space=pl.ANY)
     dma = pltpu.SemaphoreType.DMA
-    output, grad_frames, grad_qkv, grad_out = pl.pallas_call(
-        functools.partial(block_kernel, (seq_size, head_size), orders, (devices * length) ** (-0.5)),
-        out_shape=[
-            jax.ShapeDtypeStruct((length, channels), bf16),
-            jax.ShapeDtypeStruct((length, channels), bf16),
-            jax.ShapeDtypeStruct((3, tile_rows, tile_cols), f32),
-            jax.ShapeDtypeStruct((tile_rows, tile_cols), f32),
-        ],
+    shapes = [
+        jax.ShapeDtypeStruct((length, channels), bf16),
+        jax.ShapeDtypeStruct((length, channels), bf16),
+        jax.ShapeDtypeStruct((3, tile_rows, tile_cols), f32),
+        jax.ShapeDtypeStruct((tile_rows, tile_cols), f32),
+    ]
+    results = pl.pallas_call(
+        functools.partial(block_kernel, (seq_size, head_size), orders),
+        out_shape=shapes,
         in_specs=[vmem, vmem, vmem, anywhere, anywhere],
         out_specs=[vmem] * 4,
         scratch_shapes=[
             pltpu.VMEM((3, channels, channels), bf16),
             pltpu.VMEM((channels, channels), bf16),
             pltpu.VMEM((bordered, channels), bf16),
-            pltpu.VMEM((channels, length), bf16),
+            pltpu.VMEM((channels, bordered), bf16),
             pltpu.VMEM((length, channels), bf16),
             pltpu.VMEM((bordered, channels), bf16),
             pltpu.VMEM((bordered, channels), bf16),
@@ -360,10 +375,10 @@
             pltpu.VMEM((length, channels), bf16),
             pltpu.VMEM((channels, length), bf16),
             pltpu.VMEM((length, channels), bf16),
-            pltpu.VMEM((2, length, channels), f32),
-            pltpu.VMEM((pairs, 2, 2, WINDOW, wide), bf16),
-            pltpu.VMEM((pairs, 2, 2, WINDOW, wide), bf16),
-            pltpu.VMEM((2, length, channels), bf16),
+            pltpu.VMEM((2, bordered, channels), bf16),
+            pltpu.VMEM((channels // HEAD_SIZE, length // WINDOW, WINDOW, 3 * WINDOW), bf16),
+            pltpu.VMEM((2, WINDOW, channels), bf16),
+            pltpu.VMEM((2, WINDOW, channels), bf16),
             pltpu.VMEM((length, channels), f32),
             pltpu.VMEM((chunks, devices, tile_rows, tile_cols), bf16),
             pltpu.VMEM((chunks, devices, tile_rows, tile_cols), bf16),
@@ -371,8 +386,8 @@
             dma((4,)),
             dma((2,)),
             dma((2,)),
-            dma((pairs, 2)),
-            dma((pairs, 2)),
+            dma((2,)),
+            dma((2,)),
             dma((chunks, stages)),
             dma((chunks, stages)),
         ],
@@ -381,7 +396,15 @@
         ),
         name="block",
     )(frames, cotangent, norm_gain.reshape(1, channels), w_qkv, w_out)
-    return (output, grad_frames, grad_qkv, grad_out)
+    return tuple(
+        pl.pallas_call(
+            functools.partial(deliver_kernel, (devices * length) ** (-0.5)),
+            out_shape=shapes,
+            in_specs=[vmem] * 4,
+            out_specs=[vmem] * 4,
+            name="deliver",
+        )(*results)
+    )
 
 
 def solution(mesh):

time: 106 us -> 95.9 us (0.905)
  local copies, waits for them, and re-layouts: 7.07 us -> 0 us
  Pallas kernels: 98.1 us -> 95.1 us
    unnamed x4 -> x0, local copies, waits for them, and re-layouts: 7.07 us -> none
    pallas_call x1, Pallas kernels: 98.1 us -> 92.6 us  [shards(): pl.pallas_call(functools.partial(block_kernel, (seq_size, head_size), ord...]
    pallas_call x0 -> x1, Pallas kernels: none -> 2.51 us  [shards(): pl.pallas_call(functools.partial(deliver_kernel, (devices * length) ** (-...]
where the time goes in v3:
time: 95.9 us; the launch traced here: 95.7 us
  Pallas kernels  95.1 us (99%)
    pallas_call x1, Pallas kernels, shards(): pl.pallas_call(functools.partial(block_kernel, (seq_size, head_size), ord...  92.6 us
    pallas_call x1, Pallas kernels, shards(): pl.pallas_call(functools.partial(deliver_kernel, (devices * length) ** (-...  2.51 us

profile of v3, /device:TPU:0, one launch (start us, length us, event | category | flops | bytes accessed | tf_op | source)
XLA Modules:
  0.0 95.7 jit_solution(1568042298133144690)
XLA Ops:
  0.6 92.6 %block.1 = (bf16[256,1024]{1,0:T(8,128)(2,1)}, bf16[256,1024]{1,0:T(8,128)(2,1)}, f32[3,128,256]{2,1,0:T(8,128)}, f32[128,256]{1,0:T(8,128)}) custom-call(bf16[256,1024]{1,0:T(8,128)(2,1)} %frames.1, bf16[256,1024]{1,0:T(8,128)(2,1)} %cotangent.1, f32[1,1024]{1,0:T(1,128)} %bitcast.1, bf16[3,1024,1024]{2,1,0:T(8,128)(2,1)} %w_qkv_hbm.1, ...), custom_call_target="tpu_custom_call" | custom-call | tf_op jit(solution)/shard_map/block/pallas_call | solution.py:361
  93.2 2.5 %deliver.1 = (bf16[256,1024]{1,0:T(8,128)(2,1)}, bf16[256,1024]{1,0:T(8,128)(2,1)}, f32[3,128,256]{2,1,0:T(8,128)}, f32[128,256]{1,0:T(8,128)}) custom-call(bf16[256,1024]{1,0:T(8,128)(2,1)} %get-tuple-element.8.output, bf16[256,1024]{1,0:T(8,128)(2,1)} %get-tuple-element.9.grad_frames, f32[3,128,256]{2,1,0:T(8,128)} %get-tuple-element.10.grad_qkv, ...), custom_call_target="tpu_custom_call" | custom-call | tf_op jit(solution)/shard_map/deliver/pallas_call | solution.py:400

commit v4 on v3

--- a/solution.py
+++ b/solution.py
@@ -280,7 +280,9 @@
     launch(2, normed_t, grad_pair.at[0], slice(0, 2 * WINDOW + length))
     advance(1, 0)
     launch(3, normed_t, grad_pair.at[1], slice(0, 2 * WINDOW + length))
+    advance(0, 1)
     advance(2, 0)
+    advance(3, 0)
 
     def pair_back(rows, cols):
         term = dot(grad_pair[0, rows, :], w_qkv[1, cols, :], ((1,), (1,)))
@@ -292,16 +294,15 @@
             cols = slice(strip_start, strip_start + strip)
             edge_out[side, :, cols] = pair_back(slice(start, start + WINDOW), cols).astype(bf16)
         edge_copy(side).start()
-    advance(3, 0)
     for start in range(0, channels, strip):
         cols = slice(start, start + strip)
         mixed = dot(attended[...], w_out[:, cols], ((1,), (0,)))
         output[:, cols] = (frames[:, cols].astype(f32) + mixed).astype(bf16)
-    advance(0, 1)
+    advance(1, 1)
+    advance(0, 2)
     for start in range(0, channels, strip):
         cols = slice(start, start + strip)
         grad_normed[:, cols] = pair_back(own, cols) + dot(grad_query[...], w_qkv[0, cols, :], ((1,), (1,)))
-    advance(1, 1)
     advance(2, 1)
     advance(3, 1)
 
@@ -316,7 +317,7 @@
         return carry
 
     for stage in range(2, stages):
-        for chunk in range(chunks):
+        for chunk in range(1 if stage == 2 else 0, chunks):
             advance(chunk, stage)
         if stage == 2:
             edge_copy(0).wait()

time: 95.9 us -> 101 us (1.053)
  Pallas kernels: 95.1 us -> 100 us
    pallas_call x1, Pallas kernels: 92.6 us -> 97.5 us  [shards(): pl.pallas_call(functools.partial(block_kernel, (seq_size, head_size), ord...]
where the time goes in v4:
time: 101 us
  Pallas kernels  100 us (99%)
    pallas_call x1, Pallas kernels, shards(): pl.pallas_call(functools.partial(block_kernel, (seq_size, head_size), ord...  97.5 us
    pallas_call x1, Pallas kernels, shards(): pl.pallas_call(functools.partial(deliver_kernel, (devices * length) ** (-...  2.51 us

profile of v4, /device:TPU:0, one launch (start us, length us, event | category | flops | bytes accessed | tf_op | source)
XLA Modules:
  0.0 100.7 jit_solution(9757092879414368570)
XLA Ops:
  0.6 97.5 %block.1 = (bf16[256,1024]{1,0:T(8,128)(2,1)}, bf16[256,1024]{1,0:T(8,128)(2,1)}, f32[3,128,256]{2,1,0:T(8,128)}, f32[128,256]{1,0:T(8,128)}) custom-call(bf16[256,1024]{1,0:T(8,128)(2,1)} %frames.1, bf16[256,1024]{1,0:T(8,128)(2,1)} %cotangent.1, f32[1,1024]{1,0:T(1,128)} %bitcast.1, bf16[3,1024,1024]{2,1,0:T(8,128)(2,1)} %w_qkv_hbm.1, ...), custom_call_target="tpu_custom_call" | custom-call | tf_op jit(solution)/shard_map/block/pallas_call | solution.py:362
  98.2 2.5 %deliver.1 = (bf16[256,1024]{1,0:T(8,128)(2,1)}, bf16[256,1024]{1,0:T(8,128)(2,1)}, f32[3,128,256]{2,1,0:T(8,128)}, f32[128,256]{1,0:T(8,128)}) custom-call(bf16[256,1024]{1,0:T(8,128)(2,1)} %get-tuple-element.8.output, bf16[256,1024]{1,0:T(8,128)(2,1)} %get-tuple-element.9.grad_frames, f32[3,128,256]{2,1,0:T(8,128)} %get-tuple-element.10.grad_qkv, ...), custom_call_target="tpu_custom_call" | custom-call | tf_op jit(solution)/shard_map/deliver/pallas_call | solution.py:401
